TPU v7x, 512 devices: a whole 4x8x8 slice. The times are simulated.
512 devices in a mesh: dp: 8 (over z_hi, core), fsdp: 16 (over z_lo, y), tp: 4 (over x).
Axes of the slice: x: 4, y: 8, z: 8 (z_hi: 4, z_lo: 2; z = z_hi * 2 + z_lo), core: 2. Of those that a mesh axis runs over, the one named last changes fastest.
Arguments:
- layer_input: bfloat16 [65536, 4096], P(('dp', 'fsdp'), 'tp'), may hold values from -24 to 24
- value_grad: bfloat16 [65536, 2048], P(('dp', 'fsdp'), 'tp'), may hold values from -6 to 6
- residual_grad: bfloat16 [65536, 4096], P(('dp', 'fsdp'), 'tp'), may hold values from -6 to 6
- value_weight: bfloat16 [4096, 2048], P(('tp', 'fsdp')), may hold values from -0.125 to 0.125
- owner: int32 [65536, 1], P(('dp', 'fsdp')), may hold values from 0 to 15; in each aligned block of 512 rows (0 to 511, 512 to 1023, ...) at most 64 rows name the same one
- key_row: int32 [65536], P(('dp', 'fsdp')), may hold values from 0 to 255
Outputs:
- weight_grad: float32 [4096, 2048], P(('tp', 'fsdp'))
- key_grad: float32 [4096, 4096], P('fsdp', 'tp')
Inputs may be any that keep to these rules, and one draw needn't show every extreme that they name: Among the 512 tokens of one device (aligned blocks of rows) at most 64 name the same owner, and that bound is reached.
All inputs are finite; a program needn't handle non-finite values.
Results may differ from a plain program's by a relative error of at most 0.0029.
Values may be sent and summed in bfloat16 or wider, within the bound.
A program may use at most 64 MiB of HBM per device.

v0:
```python
import jax
import jax.numpy as jnp
from jax import lax
from jax.sharding import PartitionSpec as P

KEY_DEV = 256


def body(layer_input, value_grad, residual_grad, value_weight, owner, key_row):
    all_heads = lax.all_gather(value_grad, "tp", axis=1, tiled=True)
    tok_rows = layer_input.shape[0]
    features = layer_input.shape[1]
    groups = lax.axis_size("fsdp")
    slots = 2 * tok_rows // groups
    width = all_heads.shape[1]
    term = lax.dot_general(
        layer_input, all_heads, (((0,), (0,)), ((), ())), preferred_element_type=jnp.float32
    )
    pieces = term.astype(jnp.bfloat16).reshape(groups, features // groups, width)
    arrived = lax.all_to_all(pieces, "fsdp", split_axis=0, concat_axis=0, tiled=True)
    shard = jnp.sum(arrived.astype(jnp.float32), axis=0)
    back = lax.dot_general(
        all_heads,
        lax.all_gather(value_weight, "fsdp", axis=0, tiled=True),
        (((1,), (1,)), ((), ())),
        preferred_element_type=jnp.float32,
    )
    input_grad = (residual_grad.astype(jnp.float32) + back).astype(jnp.bfloat16)
    target = owner[:, 0]
    onehot = (target[:, None] == jnp.arange(groups, dtype=jnp.int32)[None, :]).astype(jnp.int32)
    position = jnp.sum(jnp.cumsum(onehot, axis=0) * onehot, axis=1) - 1
    outgoing = (
        jnp.zeros((groups, slots, features), jnp.bfloat16).at[target, position].set(input_grad)
    )
    out_keys = jnp.full((groups, slots), -1, jnp.int32).at[target, position].set(key_row)
    arrived = lax.all_to_all(outgoing, "fsdp", split_axis=0, concat_axis=0, tiled=True)
    arrived_keys = lax.all_to_all(out_keys, "fsdp", split_axis=0, concat_axis=0, tiled=True)
    flat_rows = arrived.reshape(groups * slots, features)
    selector = (
        arrived_keys.reshape(groups * slots)[:, None]
        == jnp.arange(KEY_DEV, dtype=jnp.int32)[None, :]
    ).astype(jnp.bfloat16)
    table = lax.dot_general(
        selector, flat_rows, (((0,), (0,)), ((), ())), preferred_element_type=jnp.float32
    )
    weight_grad = lax.psum(shard, "dp")
    key_grad = lax.psum(table, "dp")
    return (weight_grad, key_grad)


def solution(mesh):
    return jax.shard_map(
        body,
        mesh=mesh,
        in_specs=(
            P(("dp", "fsdp"), "tp"),
            P(("dp", "fsdp"), "tp"),
            P(("dp", "fsdp"), "tp"),
            P(("tp", "fsdp"), None),
            P(("dp", "fsdp"), None),
            P(("dp", "fsdp")),
        ),
        out_specs=(P(("tp", "fsdp"), None), P("fsdp", "tp")),
        check_vma=False,
    )
```

profile of v0, /device:TPU:1, one launch (start us, length us, event | category | flops | bytes accessed | tf_op | source)
XLA Modules:
  0.0 390.8 jit_solution(7241025913781372780)
XLA Ops:
  7.2 0.0 all-gather.3.cloned.1.call-start
  7.2 0.7 all-gather.3.cloned.1.call-update
  7.9 0.0 all-gather.5.cloned.1.call-start
  8.0 0.7 all-gather.5.cloned.1.call-update
  8.7 0.7 fusion.4
  9.4 1.1 reduce-window.6
  10.5 0.2 slice_reduce_fusion
  10.7 0.8 fusion.3
  11.5 0.7 or_select_fusion
  12.2 0.6 broadcast_in_dim.4
  12.8 70.6 %scatter_fusion = s32[16,64]{1,0:T(8,128)} fusion(s32[16,64]{1,0:T(8,128)} %broadcast_in_dim.4, s32[512]{0:T(512)S(1)} %bitcast.30, s32[512]{0:T(512)} %param.11), kind=kCustom, calls=%fused_computation | custom fusion | bytes 10240 | tf_op jit(solution)/shard_map/scatter | solution.py:35
  83.5 9.7 %all-to-all-start.1 = ((s32[16,1,64]{2,1,0:T(1,128)}), s32[16,1,64]{2,1,0:T(1,128)S(1)}, u32[]{:S(2)}, u32[]{:S(2)}) async-start(s32[16,1,64]{2,1,0:T(1,128)} %bitcast.8), calls=%async_computation.1 | async-start | bytes 16384 | tf_op jit(solution)/shard_map/all_to_all | solution.py:37
  93.2 0.0 all-gather.3.cloned.1.call-done
  93.2 6.0 %convolution_convert_fusion = bf16[1024,2048]{1,0:T(8,128)(2,1)} fusion(bf16[512,1024]{1,0:T(8,128)(2,1)S(1)} %copy-done, bf16[512,2048]{1,0:T(8,128)(2,1)} %all-gather.3.cloned.1.call-done), kind=kOutput, calls=%fused_computation.3 | convolution fusion | flops 2149580800 | bytes 7340032 | tf_op jit(solution)/shard_map/dot_general | solution.py:16
  99.2 1.3 all-to-all-done.1
  100.5 6.5 %all-to-all-start = ((bf16[16,64,2048]{2,1,0:T(8,128)(2,1)}), bf16[16,64,2048]{2,1,0:T(8,128)(2,1)}, u32[]{:S(2)}, u32[]{:S(2)}) async-start(bf16[16,64,2048]{2,1,0:T(8,128)(2,1)} %bitcast.32), calls=%async_computation | async-start | bytes 8388608 | tf_op jit(solution)/shard_map/all_to_all | solution.py:20
  107.0 51.3 %all-gather.5.cloned.1.call-done = bf16[1024,2048]{1,0:T(8,128)(2,1)} async-done(((bf16[64,2048]{1,0:T(8,128)(2,1)}), bf16[1024,2048]{1,0:T(8,128)(2,1)}) %all-gather.5.cloned.1.call-update) | async-done | bytes 4194320 | tf_op jit(solution)/shard_map/all_gather | solution.py:24
  158.3 5.2 %add_convert_fusion = bf16[512,1024]{1,0:T(8,128)(2,1)S(1)} fusion(bf16[512,1024]{1,0:T(8,128)(2,1)S(1)} %copy-done.1, bf16[512,2048]{1,0:T(8,128)(2,1)} %all-gather.3.cloned.1.call-done, bf16[1024,2048]{1,0:T(8,128)(2,1)} %all-gather.5.cloned.1.call-done), kind=kOutput, calls=%fused_computation.4 | convolution fusion | flops 2149056512 | bytes 8388608 | tf_op jit(solution)/shard_map/dot_general | solution.py:22
  163.5 1.7 broadcast_in_dim.5
  165.1 73.0 %scatter_fusion.1 = bf16[16,64,1024]{2,1,0:T(8,128)(2,1)} fusion(bf16[16,64,1024]{2,1,0:T(8,128)(2,1)} %broadcast_in_dim.5, s32[512]{0:T(512)S(1)} %bitcast.31, bf16[512,1024]{1,0:T(8,128)(2,1)S(1)} %add_convert_fusion), kind=kCustom, calls=%fused_computation.1 | custom fusion | bytes 3149824 | tf_op jit(solution)/shard_map/scatter | solution.py:33
  238.2 3.7 all-to-all-start.2
  241.9 0.0 all-reduce.3.cloned.1.call-start
  241.9 0.5 broadcast.102
  242.4 0.7 reduce.5
  243.1 0.1 eq.48
  243.2 3.8 convert_reduce_fusion
  247.0 22.4 %all-to-all-done.2 = bf16[16,64,1024]{2,1,0:T(8,128)(2,1)S(1)} async-done(((bf16[16,64,1024]{2,1,0:T(8,128)(2,1)}), bf16[16,64,1024]{2,1,0:T(8,128)(2,1)S(1)}, u32[]{:S(2)}, u32[]{:S(2)}) %all-to-all-start.2) | async-done | bytes 2097184 | tf_op jit(solution)/shard_map/all_to_all | solution.py:36
  269.3 1.9 fusion
  271.3 0.0 all-reduce.3.cloned.1.call-update
  271.3 108.8 %all-reduce.3.cloned.1.call-done = (f32[64,2048]{1,0:T(8,128)}, f32[256,1024]{1,0:T(8,128)}) async-done(((f32[64,2048]{1,0:T(8,128)}, f32[256,1024]{1,0:T(8,128)}), (f32[64,2048]{1,0:T(8,128)}, f32[256,1024]{1,0:T(8,128)})) %all-reduce.3.cloned.1.call-update) | async-done | bytes 1572880 | tf_op jit(solution)/shard_map/psum | solution.py:46
  380.1 1.9 copy.17
  382.0 2.3 copy.18
  (8 shorter events, 0.1 us)
Async XLA Ops:
  7.2 86.1 %copy-start = (bf16[512,1024]{1,0:T(8,128)(2,1)S(1)}, bf16[512,1024]{1,0:T(8,128)(2,1)}, u32[]{:S(2)}) copy-start(bf16[512,1024]{1,0:T(8,128)(2,1)} %param.6) | copy-start | bytes 3145732
  7.2 86.1 %all-gather.3.cloned.1.call-start = ((), (), s32[]{:S(2)}) async-start(), calls=%async_computation.3 | async-start | bytes 2621440 | tf_op jit(solution)/shard_map/all_gather | solution.py:10
  7.9 150.3 %all-gather.5.cloned.1.call-start = ((), (), s32[]{:S(2)}) async-start(), calls=%async_computation.4 | async-start | bytes 4456448 | tf_op jit(solution)/shard_map/all_gather | solution.py:24
  83.5 17.0 %all-to-all-start.1 = ((s32[16,1,64]{2,1,0:T(1,128)}), s32[16,1,64]{2,1,0:T(1,128)S(1)}, u32[]{:S(2)}, u32[]{:S(2)}) async-start(s32[16,1,64]{2,1,0:T(1,128)} %bitcast.8), calls=%async_computation.1 | async-start | bytes 16384 | tf_op jit(solution)/shard_map/all_to_all | solution.py:37
  100.5 57.8 %copy-start.1 = (bf16[512,1024]{1,0:T(8,128)(2,1)S(1)}, bf16[512,1024]{1,0:T(8,128)(2,1)}, u32[]{:S(2)}) copy-start(bf16[512,1024]{1,0:T(8,128)(2,1)} %param.8) | copy-start | bytes 3145732
  100.5 137.7 %all-to-all-start = ((bf16[16,64,2048]{2,1,0:T(8,128)(2,1)}), bf16[16,64,2048]{2,1,0:T(8,128)(2,1)}, u32[]{:S(2)}, u32[]{:S(2)}) async-start(bf16[16,64,2048]{2,1,0:T(8,128)(2,1)} %bitcast.32), calls=%async_computation | async-start | bytes 8388608 | tf_op jit(solution)/shard_map/all_to_all | solution.py:20
  238.2 31.2 %all-to-all-start.2 = ((bf16[16,64,1024]{2,1,0:T(8,128)(2,1)}), bf16[16,64,1024]{2,1,0:T(8,128)(2,1)S(1)}, u32[]{:S(2)}, u32[]{:S(2)}) async-start(bf16[16,64,1024]{2,1,0:T(8,128)(2,1)} %scatter_fusion.1), calls=%async_computation.2 | async-start | bytes 4194304 | tf_op jit(solution)/shard_map/all_to_all | solution.py:36
  241.9 138.2 %all-reduce.3.cloned.1.call-start = ((), (), s32[]{:S(2)}) async-start(), calls=%async_computation.5 | async-start | bytes 3145728 | tf_op jit(solution)/shard_map/psum | solution.py:46
Sparse Core Ops, SparseCore 0:
  10.1 41.3 all-gather.2
  53.6 104.6 all-gather.4
  271.4 108.6 all-reduce.2
where the time goes:
time: 395 us; the launch traced here: 391 us
  waiting for transfers between devices  185 us (47%)
  local copies, waits for them, and re-layouts  151 us (38%)
  starting transfers between devices  20.1 us (5%)
  between operations  13.8 us (3%)
  matrix products  13.1 us (3%)
  other arithmetic  7.81 us (2%)
    psum x1, waiting for transfers between devices, body(): weight_grad = lax.psum(shard, 'dp')  109 us
    scatter x1, local copies, waits for them, and re-layouts, body(): jnp.zeros((groups, slots, features), jnp.bfloat16).at[target, position]  73 us
    scatter x1, local copies, waits for them, and re-layouts, body(): jnp.full((groups, slots), -1, jnp.int32).at[target, position].set(key_row)  70.6 us
    all_gather x1, waiting for transfers between devices, body(): lax.all_gather(value_weight, 'fsdp', axis=0, tiled=True)  51.3 us
    all_to_all x1, waiting for transfers between devices, body(): lax.all_to_all(outgoing, 'fsdp', split_axis=0, concat_axis=0, tiled=True)  22.4 us
    all_to_all x1, starting transfers between devices, body(): lax.all_to_all(out_keys, 'fsdp', split_axis=0, concat_axis=0, tiled=True)  9.75 us
  transfers between devices with their start and end apart: 6, of which 4 were waited for; matrix products, arithmetic and copies ran while one was open for 42% of the time, Pallas kernels for 0%

commit v1 on v0

v1 whole, which is shorter than its diff:
```python
import jax
import jax.numpy as jnp
from jax import lax
from jax.experimental import pallas as pl
from jax.experimental.pallas import tpu as pltpu
from jax.sharding import PartitionSpec as P

MESH = pl.DeviceIdType.MESH
BF, F32 = jnp.bfloat16, jnp.float32
NX, NY, NZ, NH = 4, 8, 8, 4
TOK, FEAT, HEADS, WIDTH = 512, 512, 512, 2048
SLOTS, KEYS, ROWS, COLS = 64, 256, 64, 256
HALF = TOK // 2


def dot(a, b, dims):
    return lax.dot_general(a, b, (dims, ((), ())), preferred_element_type=F32)


def kernel(
    li_ref, vgr_ref, res_ref, wsh_ref, own_ref, key_ref,
    wout, kout,
    vg, li2, res_p, own_p, key_p, w, wp, wr, ws, yr, wf, acc, igb, pk, km, kr, kmr, table, tb, zr, kf,
    loc, p_s, p_r, x_s, x_r, v_s, v_r, wy_s, wy_r, wz_s, wz_r,
    a_s, a_r, k_s, k_r, m_s, m_r, b_s, b_r, z_s, z_r, d_s, d_r, e_s, e_r, f_s, f_r, g_s, g_r,
):
    dp, fs, x = lax.axis_index("dp"), lax.axis_index("fsdp"), lax.axis_index("tp")
    zh, c, zl, y = dp // 2, dp % 2, fs // NY, fs % NY
    z = zh * 2 + zl
    near = zl == c
    far = zl != c

    def at(x_=x, y_=y, z_=z, c_=c):
        return ((z_ // 2) * 2 + c_, (z_ % 2) * NY + y_, x_)

    partner = at(c_=1 - c)
    right, left = (x + 1) % NX, (x + NX - 1) % NX
    ended = []

    def send(src, dst, ss, rs, to, later=True):
        pltpu.make_async_remote_copy(
            src_ref=src, dst_ref=dst, send_sem=ss, recv_sem=rs, device_id=to, device_id_type=MESH
        ).start()
        if later:
            ended.append((src, ss))

    def got(dst, rs):
        pltpu.make_async_copy(dst, dst, rs).wait()

    def cols(i):
        return pl.ds(pl.multiple_of(i * HEADS, HEADS), HEADS)

    def mine(i):
        return pl.ds(pl.multiple_of(i * FEAT, FEAT), FEAT)

    def shard(i, start=0, size=ROWS):
        return pl.ds(pl.multiple_of(i * ROWS + start, 32), size)

    barrier = pltpu.get_barrier_semaphore()
    peers = [partner, at(x_=right), at(x_=left)]
    peers += [at(y_=(y + d) % NY) for d in range(1, NY)] + [at(z_=(z + d) % NZ) for d in range(1, NZ)]
    for peer in peers:
        pl.semaphore_signal(barrier, inc=1, device_id=peer, device_id_type=MESH)
    pl.semaphore_wait(barrier, len(peers))

    top, low = pl.ds(0, HALF), pl.ds(HALF, HALF)
    send(vgr_ref.at[top], vg.at[0, top, cols(x)], x_s.at[0], x_r.at[0], at(x_=right))
    send(vgr_ref.at[low], vg.at[0, low, cols(x)], x_s.at[2], x_r.at[2], at(x_=left))
    send(vgr_ref.at[low], vg.at[0, low, cols(x)], x_s.at[1], x_r.at[1], at(x_=right))
    send(vgr_ref.at[top], vg.at[0, top, cols(x)], x_s.at[3], x_r.at[3], at(x_=left))

    up, down = at(z_=(z + 1) % NZ), at(z_=(z + NZ - 1) % NZ)
    after, before = at(y_=(y + 1) % NY), at(y_=(y + NY - 1) % NY)

    @pl.when(near)
    def _():
        send(wsh_ref, w.at[shard(y)], wy_s.at[0], wy_r.at[0], after, False)
        send(wsh_ref, w.at[shard(y)], wy_s.at[4], wy_r.at[4], before, False)
        send(wsh_ref.at[pl.ds(0, 32)], w.at[shard(y, 0, 32)], wz_s.at[0], wz_r.at[0], up, False)
        send(wsh_ref.at[pl.ds(32, 32)], w.at[shard(y, 32, 32)], wz_s.at[1], wz_r.at[1], down, False)
        pltpu.make_async_copy(wsh_ref, w.at[shard(y)], loc.at[2]).start()

    send(vgr_ref, vg.at[1, :, cols(x)], v_s.at[0], v_r.at[0], partner)
    send(li_ref.at[:, mine(1 - c)], li2.at[1], p_s.at[0], p_r.at[0], partner)
    send(own_ref, own_p, p_s.at[1], p_r.at[1], partner)
    send(key_ref, key_p, p_s.at[2], p_r.at[2], partner)
    send(res_ref.at[:, mine(1 - c)], res_p, p_s.at[3], p_r.at[3], partner)
    own_vg = pltpu.make_async_copy(vgr_ref, vg.at[0, :, cols(x)], loc.at[0])
    own_vg.start()
    own_li = pltpu.make_async_copy(li_ref.at[:, mine(c)], li2.at[0], loc.at[1])
    own_li.start()

    def weights(k):
        plus, minus = (y + NY - k) % NY, (y + k) % NY
        got(w.at[shard(plus)], wy_r.at[k - 1])
        part = (0, 32) if k == 3 else (0, ROWS)
        send(w.at[shard(plus, *part)], w.at[shard(plus, *part)], wy_s.at[k], wy_r.at[k], after, False)
        send(w.at[shard(plus)], w.at[shard(plus)], wz_s.at[1 + k], wz_r.at[1 + k], down, False)
        got(w.at[shard(minus)], wy_r.at[3 + k])
        part = (32, 32) if k == 3 else (0, ROWS)
        send(w.at[shard(minus, *part)], w.at[shard(minus, *part)], wy_s.at[4 + k], wy_r.at[4 + k], before, False)
        send(w.at[shard(minus)], w.at[shard(minus)], wz_s.at[4 + k], wz_r.at[4 + k], up, False)

    def places(owner):
        hot = (lax.broadcasted_iota(jnp.int32, (16, TOK), 0) == owner).astype(F32)
        order = lax.broadcasted_iota(jnp.int32, (TOK, TOK), 0) <= lax.broadcasted_iota(jnp.int32, (TOK, TOK), 1)
        count = dot(hot.astype(BF), order.astype(F32).astype(BF), ((1,), (0,)))
        rank = jnp.sum(count * hot, axis=0, keepdims=True) - 1.0
        return owner * SLOTS + rank.astype(jnp.int32)

    slot = [places(own_ref[...]), None]

    @pl.when(near)
    def _():
        weights(1)

    got(vg.at[0, top, cols(left)], x_r.at[0])
    send(vg.at[0, top, cols(left)], vg.at[0, top, cols(left)], x_s.at[4], x_r.at[4], at(x_=right))
    send(vg.at[0, top, cols(left)], vg.at[1, top, cols(left)], v_s.at[1], v_r.at[1], partner)
    got(vg.at[0, low, cols(right)], x_r.at[2])
    send(vg.at[0, low, cols(right)], vg.at[0, low, cols(right)], x_s.at[5], x_r.at[5], at(x_=left))
    send(vg.at[0, low, cols(right)], vg.at[1, low, cols(right)], v_s.at[2], v_r.at[2], partner)

    @pl.when(near)
    def _():
        weights(2)

    def weight_tile(q):
        total = None
        for b in range(2):
            part = dot(li2[b], vg[b, :, cols(q)], ((0,), (0,))).astype(BF).astype(F32)
            total = part if total is None else total + part
        total = total.astype(BF)
        wp[2 * q] = total[:, :COLS]
        wp[2 * q + 1] = total[:, COLS:]

    own_vg.wait()
    own_li.wait()
    got(li2.at[1], p_r.at[0])
    got(vg.at[1, :, cols(x)], v_r.at[0])
    weight_tile(x)

    @pl.when(near)
    def _():
        weights(3)

    got(vg.at[0, low, cols(left)], x_r.at[1])
    send(vg.at[0, low, cols(left)], vg.at[1, low, cols(left)], v_s.at[3], v_r.at[3], partner)
    got(vg.at[0, top, cols(right)], x_r.at[3])
    send(vg.at[0, top, cols(right)], vg.at[1, top, cols(right)], v_s.at[4], v_r.at[4], partner)

    opposite = (y + 4) % NY

    @pl.when(near)
    def _():
        got(w.at[shard(opposite, 0, 32)], wy_r.at[3])
        send(w.at[shard(opposite, 0, 32)], w.at[shard(opposite, 0, 32)], wz_s.at[8], wz_r.at[8], up, False)
        got(w.at[shard(opposite, 32, 32)], wy_r.at[7])
        send(w.at[shard(opposite, 32, 32)], w.at[shard(opposite, 32, 32)], wz_s.at[9], wz_r.at[9], down, False)

    got(own_p, p_r.at[1])
    got(key_p, p_r.at[2])
    slot[1] = places(own_p[...])

    got(vg.at[1, top, cols(left)], v_r.at[1])
    got(vg.at[1, low, cols(left)], v_r.at[3])
    weight_tile(left)

    across = (x + 2) % NX
    got(vg.at[0, top, cols(across)], x_r.at[4])
    send(vg.at[0, top, cols(across)], vg.at[1, top, cols(across)], v_s.at[5], v_r.at[5], partner)
    got(vg.at[0, low, cols(across)], x_r.at[5])
    send(vg.at[0, low, cols(across)], vg.at[1, low, cols(across)], v_s.at[6], v_r.at[6], partner)

    got(vg.at[1, low, cols(right)], v_r.at[2])
    got(vg.at[1, top, cols(right)], v_r.at[4])
    weight_tile(right)

    @pl.when(near)
    def _():
        pltpu.make_async_copy(wsh_ref, w.at[shard(y)], loc.at[2]).wait()

    @pl.when(far)
    def _():
        got(w.at[shard(y, 0, 32)], wz_r.at[0])
        got(w.at[shard(y, 32, 32)], wz_r.at[1])
        for k in range(1, 4):
            got(w.at[shard((y + NY - k) % NY)], wz_r.at[1 + k])
            got(w.at[shard((y + k) % NY)], wz_r.at[4 + k])
        got(w.at[shard(opposite, 0, 32)], wz_r.at[8])
        got(w.at[shard(opposite, 32, 32)], wz_r.at[9])

    got(res_p, p_r.at[3])
    acc[0] = res_ref[:, mine(c)].astype(F32)
    acc[1] = res_p[...].astype(F32)

    def back_tile(q):
        for b in range(2):
            acc[b] += dot(vg[b, :, cols(q)], w[:, cols(q)], ((1,), (1,)))

    back_tile(x)
    back_tile(left)
    back_tile(right)
    got(vg.at[1, top, cols(across)], v_r.at[5])
    got(vg.at[1, low, cols(across)], v_r.at[6])
    back_tile(across)
    igb[...] = acc[...].astype(BF)

    line = lax.broadcasted_iota(jnp.int32, (2 * SLOTS, 1), 0)
    keys = [jnp.broadcast_to((ref[...] + 1).astype(F32), (8, TOK)).astype(BF) for ref in (key_ref, key_p)]

    def pack(d):
        to = (y + d) % NY
        wanted = (line // SLOTS) * (NY * SLOTS) + to * SLOTS + line % SLOTS
        for b in range(2):
            pick = (wanted == slot[b]).astype(F32).astype(BF)
            pk[d, pl.ds(b * 2 * SLOTS, 2 * SLOTS)] = dot(pick, igb[b], ((1,), (0,))).astype(BF)
            km[d, :, pl.ds(b * 2 * SLOTS, 2 * SLOTS)] = dot(keys[b], pick, ((1,), (1,)))
        if d > 0:
            send(pk.at[d], kr.at[d], k_s.at[d], k_r.at[d], at(y_=to))
            send(km.at[d], kmr.at[d], m_s.at[d], m_r.at[d], at(y_=to))

    for d in (4, 3, 5, 2, 6, 1, 7, 0):
        pack(d)

    weight_tile(across)
    for d in (4, 3, 5, 2, 6, 1, 7):
        to = (z + d) % NZ
        send(wp.at[to], wr.at[d], a_s.at[d], a_r.at[d], at(z_=to))

    lane = lax.broadcasted_iota(jnp.int32, (1, 4 * SLOTS), 1)
    offset = ((lane // SLOTS) % 2) * KEYS - 1

    def tally(d, rows, marks):
        named = marks[d, 0:1, :].astype(jnp.int32)
        number = jnp.where(named > 0, named + offset, -1)
        hit = (lax.broadcasted_iota(jnp.int32, (2 * KEYS, 4 * SLOTS), 0) == number).astype(F32).astype(BF)
        return dot(hit, rows[d], ((1,), (0,)))

    table[...] = tally(0, pk, km)
    for d in (1, 7, 2, 6, 3, 5, 4):
        got(kr.at[d], k_r.at[d])
        got(kmr.at[d], m_r.at[d])
        table[...] += tally(d, kr, kmr)
    tb[...] = table[...].astype(BF)

    def piece(place):
        return pl.ds(pl.multiple_of(((place % 2) * NH + place // 2) * ROWS, ROWS), ROWS)

    for d in (4, 3, 5, 2, 6, 1, 7):
        to = (z + d) % NZ
        send(tb.at[piece(to)], zr.at[d], z_s.at[d], z_r.at[d], at(z_=to))

    for d in (1, 7, 2, 6, 3, 5, 4):
        got(wr.at[d], a_r.at[d])

    @pl.loop(0, NY)
    def _(i):
        rows = pl.ds(pl.multiple_of(i * ROWS, ROWS), ROWS)
        total = wp[z, rows].astype(F32)
        for d in range(1, NZ):
            total = total + wr[d, rows].astype(F32)
        ws[i] = total.astype(BF)

    for d in (4, 3, 5, 2, 6, 1, 7):
        to = (y + d) % NY
        send(ws.at[to], yr.at[d], b_s.at[d], b_r.at[d], at(y_=to))

    total = table[piece(z), :]
    for d in (1, 7, 2, 6, 3, 5, 4):
        got(zr.at[d], z_r.at[d])
        total = total + zr[d].astype(F32)
    kf[...] = total

    def block(i):
        return pl.ds(pl.multiple_of(i * ROWS, ROWS), ROWS)

    for e in (2, 1, 3):
        send(kf, kout.at[block(zh), mine(c)], d_s.at[e], d_r.at[e], at(z_=((zh + e) % NH) * 2 + zl))
    send(kf, kout.at[block(zh), mine(c)], e_s.at[0], e_r.at[0], partner)
    kout[block(zh), mine(c)] = total

    total = ws[y].astype(F32)
    for d in (1, 7, 2, 6, 3, 5, 4):
        got(yr.at[d], b_r.at[d])
        total = total + yr[d].astype(F32)
    wf[...] = total

    def strip(i):
        return pl.ds(pl.multiple_of(i * COLS, COLS), COLS)

    for e in (2, 1, 3):
        send(wf, wout.at[:, strip(z)], f_s.at[e], f_r.at[z], at(z_=((zh + e) % NH) * 2 + c))

    @pl.when(far)
    def _():
        send(wf, wout.at[:, strip(z)], f_s.at[0], f_r.at[z], at(z_=zh * 2 + c), False)

    @pl.when(near)
    def _():
        wout[:, strip(z)] = wf[...]
        send(wf, wout.at[:, strip(z)], g_s.at[0], g_r.at[0], partner, False)

    for e in (1, 3, 2):
        source = (zh + NH - e) % NH
        here = kout.at[block(source), mine(c)]
        got(here, d_r.at[e])
        send(here, here, e_s.at[e], e_r.at[e], partner)

    @pl.when(near)
    def _():
        for d in (1, 7, 2, 6, 3, 5, 4):
            here = wout.at[:, strip((z + d) % NZ)]
            got(here, f_r.at[(z + d) % NZ])
            send(here, here, g_s.at[d], g_r.at[d], partner, False)

    @pl.when(far)
    def _():
        for d in range(NZ):
            got(wout.at[:, strip((z + d) % NZ)], g_r.at[d])

    for e in range(NH):
        got(kout.at[block((zh + NH - e) % NH), mine(1 - c)], e_r.at[e])

    for src, sem in ended:
        got(src, sem)

    @pl.when(near)
    def _():
        for k in (0, 1, 2, 4, 5, 6):
            got(wsh_ref, wy_s.at[k])
        for k in (3, 7):
            got(wsh_ref.at[pl.ds(0, 32)], wy_s.at[k])
        for k in range(2, 8):
            got(wsh_ref, wz_s.at[k])
        for k in (0, 1, 8, 9):
            got(wsh_ref.at[pl.ds(0, 32)], wz_s.at[k])
        for d in range(NZ):
            got(wf, g_s.at[d])

    @pl.when(far)
    def _():
        got(wf, f_s.at[0])


def body(layer_input, value_grad, residual_grad, value_weight, owner, key_row):
    dma = pltpu.SemaphoreType.DMA
    vmem = pl.BlockSpec(memory_space=pltpu.VMEM)
    scratch = [
        pltpu.VMEM((2, TOK, WIDTH), BF),
        pltpu.VMEM((2, TOK, FEAT), BF),
        pltpu.VMEM((TOK, FEAT), BF),
        pltpu.VMEM((1, TOK), jnp.int32),
        pltpu.VMEM((1, TOK), jnp.int32),
        pltpu.VMEM((FEAT, WIDTH), BF),
        pltpu.VMEM((NZ, FEAT, COLS), BF),
        pltpu.VMEM((NZ, FEAT, COLS), BF),
        pltpu.VMEM((NY, ROWS, COLS), BF),
        pltpu.VMEM((NY, ROWS, COLS), BF),
        pltpu.VMEM((ROWS, COLS), F32),
        pltpu.VMEM((2, TOK, FEAT), F32),
        pltpu.VMEM((2, TOK, FEAT), BF),
        pltpu.VMEM((NY, 4 * SLOTS, FEAT), BF),
        pltpu.VMEM((NY, 8, 4 * SLOTS), F32),
        pltpu.VMEM((NY, 4 * SLOTS, FEAT), BF),
        pltpu.VMEM((NY, 8, 4 * SLOTS), F32),
        pltpu.VMEM((2 * KEYS, FEAT), F32),
        pltpu.VMEM((2 * KEYS, FEAT), BF),
        pltpu.VMEM((NZ, ROWS, FEAT), BF),
        pltpu.VMEM((ROWS, FEAT), F32),
        dma((3,)),
    ]
    for number in (4, 6, 7, 8, 10, 8, 8, 8, 8, 8, 4, 4):
        scratch += [dma((number,)), dma((number,))]
    scratch += [dma((4,)), dma((8,)), dma((8,)), dma((8,))]
    return pl.pallas_call(
        kernel,
        out_shape=(
            jax.ShapeDtypeStruct((ROWS, WIDTH), F32),
            jax.ShapeDtypeStruct((KEYS, 2 * FEAT), F32),
        ),
        in_specs=[vmem] * 6,
        out_specs=(vmem, vmem),
        scratch_shapes=scratch,
        compiler_params=pltpu.CompilerParams(
            collective_id=0, has_side_effects=True, vmem_limit_bytes=60 * 1024 * 1024
        ),
    )(layer_input, value_grad, residual_grad, value_weight, owner.reshape(1, TOK), key_row.reshape(1, TOK))


def solution(mesh):
    return jax.shard_map(
        body,
        mesh=mesh,
        in_specs=(
            P(("dp", "fsdp"), "tp"),
            P(("dp", "fsdp"), "tp"),
            P(("dp", "fsdp"), "tp"),
            P(("tp", "fsdp"), None),
            P(("dp", "fsdp"), None),
            P(("dp", "fsdp")),
        ),
        out_specs=(P(("tp", "fsdp"), None), P("fsdp", "tp")),
        check_vma=False,
    )
```

time: 395 us -> 131 us (0.33)
  waiting for transfers between devices: 185 us -> 0 us
  local copies, waits for them, and re-layouts: 151 us -> 2.93 us
  Pallas kernels: 0 us -> 127 us
  starting transfers between devices: 20.1 us -> 0 us
  between operations: 13.8 us -> 0.65 us
  matrix products: 13.1 us -> 0 us
  other arithmetic: 7.81 us -> 0 us
    scatter x2 -> x0, local copies, waits for them, and re-layouts: 144 us -> none  [the longest x1 73 us: body(): jnp.zeros((groups, slots, features), jnp.bfloat16).at[target, position]]
    pallas_call x0 -> x1, Pallas kernels: none -> 127 us  [body(): pl.pallas_call(kernel, out_shape=(jax.ShapeDtypeStruct((ROWS, WIDTH), F32...]
    psum x1 -> x0, waiting for transfers between devices: 109 us -> none  [body(): weight_grad = lax.psum(shard, 'dp')]
    all_gather x2 -> x0, waiting for transfers between devices: 51.3 us -> none  [the longest x1 51.3 us: body(): lax.all_gather(value_weight, 'fsdp', axis=0, tiled=True)]
    all_to_all x3 -> x0, waiting for transfers between devices: 23.6 us -> none  [the longest x1 22.4 us: body(): lax.all_to_all(outgoing, 'fsdp', split_axis=0, concat_axis=0, tiled=True)]
    all_to_all x3 -> x0, starting transfers between devices: 19.9 us -> none  [the longest x1 9.75 us: body(): lax.all_to_all(out_keys, 'fsdp', split_axis=0, concat_axis=0, tiled=True)]
    dot_general x3 -> x0, matrix products: 13.1 us -> none  [the longest x1 5.97 us: body(): lax.dot_general(layer_input, all_heads, (((0,), (0,)), ((), ())), preferr...]
    reduce_sum x2 -> x0, other arithmetic: 4.58 us -> none  [the longest x1 3.8 us: body(): shard = jnp.sum(arrived.astype(jnp.float32), axis=0)]
  transfers between devices with their start and end apart: 6 -> 0, of which waited for: 4 -> 0; matrix products, arithmetic and copies ran while one was open for 42% -> 0% of each run, Pallas kernels for 0% -> 0%
where the time goes in v1:
time: 131 us
  Pallas kernels  127 us (97%)
  local copies, waits for them, and re-layouts  2.93 us (2%)
    pallas_call x1, Pallas kernels, body(): pl.pallas_call(kernel, out_shape=(jax.ShapeDtypeStruct((ROWS, WIDTH), F32...  127 us
    unnamed x4, local copies, waits for them, and re-layouts  2.93 us

profile of v1, /device:TPU:1, one launch (start us, length us, event | category | flops | bytes accessed | tf_op | source)
XLA Modules:
  0.0 130.5 jit_solution(3683519989492690488)
XLA Ops:
  0.6 126.9 %shard_map.77 = (f32[64,2048]{1,0:T(8,128)}, f32[256,1024]{1,0:T(8,128)}) custom-call(bf16[512,1024]{1,0:T(8,128)(2,1)} %li_ref.1, bf16[512,512]{1,0:T(8,128)(2,1)} %vgr_ref.1, bf16[512,1024]{1,0:T(8,128)(2,1)} %res_ref.1, bf16[64,2048]{1,0:T(8,128)(2,1)} %wsh_ref.1, s32[1,512]{1,0:T(1,128)} %bitcast.2, s32[1,512]{1,0:T(1,128)} %bitcast.3), custom_call_target="tpu_custom_call" | custom-call | tf_op jit(solution)/shard_map/pallas_call | solution.py:376
  127.6 0.0 copy-start
  127.6 2.0 %copy.10 = f32[64,2048]{1,0:T(8,128)} copy(f32[64,2048]{1,0:T(8,128)} %get-tuple-element.4) | data formatting | bytes 1048576
  129.5 0.0 copy-done
  129.6 1.0 copy.11
Async XLA Ops:
  127.6 2.0 %copy-start = (f32[256,1024]{1,0:T(8,128)S(1)}, f32[256,1024]{1,0:T(8,128)}, u32[]{:S(2)}) copy-start(f32[256,1024]{1,0:T(8,128)} %get-tuple-element.5) | copy-start | bytes 3145732

commit v2 on v1

v2 whole, which is shorter than its diff:
```python
import jax
import jax.numpy as jnp
from jax import lax
from jax.experimental import pallas as pl
from jax.experimental.pallas import tpu as pltpu
from jax.sharding import PartitionSpec as P

MESH = pl.DeviceIdType.MESH
BF, F32 = jnp.bfloat16, jnp.float32
NX, NY, NZ, NH = 4, 8, 8, 4
TOK, FEAT, HEADS, WIDTH = 512, 512, 512, 2048
SLOTS, KEYS, ROWS, COLS = 64, 256, 64, 256
HALF = TOK // 2
PART = FEAT // 2
ORDER = (4, 3, 5, 2, 6, 1, 7)


def dot(a, b, dims):
    return lax.dot_general(a, b, (dims, ((), ())), preferred_element_type=F32)


def kernel(
    li_ref, vgr_ref, res_ref, wsh_ref, own_ref, key_ref,
    wout, kout,
    vg, li2, res2, own_p, key_p, w, wp, cr, cs, cfs, cfr, ctot, ws, yr, wf, acc, igb, pk, km, kr, kmr, table, tb, zr, kb,
    loc, p_s, p_r, x_s, x_r, v_s, v_r, wy_s, wy_r, wz_s, wz_r,
    c_s, c_r, k_s, k_r, m_s, m_r, b_s, b_r, z_s, z_r, d_s, d_r, e_s, e_r, f_s, f_r, g_s, g_r,
):
    dp, fs, x = lax.axis_index("dp"), lax.axis_index("fsdp"), lax.axis_index("tp")
    zh, c, zl, y = dp // 2, dp % 2, fs // NY, fs % NY
    z = zh * 2 + zl
    near = zl == c
    far = zl != c

    def at(x_=x, y_=y, z_=z, c_=c):
        return ((z_ // 2) * 2 + c_, (z_ % 2) * NY + y_, x_)

    partner = at(c_=1 - c)
    right, left = (x + 1) % NX, (x + NX - 1) % NX
    ended = []

    def send(src, dst, ss, rs, to, later=True):
        pltpu.make_async_remote_copy(
            src_ref=src, dst_ref=dst, send_sem=ss, recv_sem=rs, device_id=to, device_id_type=MESH
        ).start()
        if later:
            ended.append((src, ss))

    def got(dst, rs):
        pltpu.make_async_copy(dst, dst, rs).wait()

    def cols(i):
        return pl.ds(pl.multiple_of(i * HEADS, HEADS), HEADS)

    def mine(i):
        return pl.ds(pl.multiple_of(i * FEAT, FEAT), FEAT)

    def half(i, h):
        return pl.ds(pl.multiple_of(i * ROWS + h * 32, 32), 32)

    def block(i):
        return pl.ds(pl.multiple_of(i * ROWS, ROWS), ROWS)

    barrier = pltpu.get_barrier_semaphore()
    peers = [partner, at(x_=right), at(x_=left)]
    peers += [at(y_=(y + d) % NY) for d in range(1, NY)] + [at(z_=(z + d) % NZ) for d in range(1, NZ)]
    for peer in peers:
        pl.semaphore_signal(barrier, inc=1, device_id=peer, device_id_type=MESH)

    own_vg = pltpu.make_async_copy(vgr_ref, vg.at[0, :, cols(x)], loc.at[0])
    own_vg.start()
    own_li = pltpu.make_async_copy(li_ref.at[:, mine(c)], li2.at[0], loc.at[1])
    own_li.start()
    own_res = pltpu.make_async_copy(res_ref.at[:, mine(c)], res2.at[0], loc.at[2])
    own_res.start()

    @pl.when(near)
    def _():
        pltpu.make_async_copy(wsh_ref, w.at[block(y)], loc.at[3]).start()

    pl.semaphore_wait(barrier, len(peers))

    up, down = at(z_=(z + 1) % NZ), at(z_=(z + NZ - 1) % NZ)
    after, before = at(y_=(y + 1) % NY), at(y_=(y + NY - 1) % NY)
    first, second = pl.ds(0, 32), pl.ds(32, 32)

    @pl.when(near)
    def _():
        for h, rows in enumerate((first, second)):
            send(wsh_ref.at[rows], w.at[half(y, h)], wy_s.at[h], wy_r.at[h], after, False)
            send(wsh_ref.at[rows], w.at[half(y, h)], wy_s.at[8 + h], wy_r.at[8 + h], before, False)
        send(wsh_ref.at[first], w.at[half(y, 0)], wz_s.at[0], wz_r.at[0], up, False)
        send(wsh_ref.at[second], w.at[half(y, 1)], wz_s.at[8], wz_r.at[8], down, False)

    top, low = pl.ds(0, HALF), pl.ds(HALF, HALF)
    send(vgr_ref.at[top], vg.at[0, top, cols(x)], x_s.at[0], x_r.at[0], at(x_=right))
    send(vgr_ref.at[low], vg.at[0, low, cols(x)], x_s.at[2], x_r.at[2], at(x_=left))
    send(vgr_ref.at[low], vg.at[0, low, cols(x)], x_s.at[1], x_r.at[1], at(x_=right))
    send(vgr_ref.at[top], vg.at[0, top, cols(x)], x_s.at[3], x_r.at[3], at(x_=left))
    send(vgr_ref, vg.at[1, :, cols(x)], v_s.at[0], v_r.at[0], partner)
    send(li_ref.at[:, mine(1 - c)], li2.at[1], p_s.at[0], p_r.at[0], partner)
    send(own_ref, own_p, p_s.at[1], p_r.at[1], partner)
    send(key_ref, key_p, p_s.at[2], p_r.at[2], partner)
    send(res_ref.at[:, mine(1 - c)], res2.at[1], p_s.at[3], p_r.at[3], partner)

    def weights(k):
        plus, minus = (y + NY - k) % NY, (y + k) % NY
        for h in range(2):
            for base, shard, onward, side, keeps in ((0, plus, after, down, 0), (8, minus, before, up, 1)):
                if k == 4 and h != keeps:
                    continue
                here = w.at[half(shard, h)]
                got(here, wy_r.at[base + 2 * (k - 1) + h])
                if k < 3 or (k == 3 and h == keeps):
                    send(here, here, wy_s.at[base + 2 * k + h], wy_r.at[base + 2 * k + h], onward, False)
                if k < 4:
                    number = (8 if base == 0 else 0) + 2 * k - 1 + h
                    send(here, here, wz_s.at[number], wz_r.at[number], side, False)
                else:
                    number = 7 if base == 0 else 15
                    send(here, here, wz_s.at[number], wz_r.at[number], up if base == 0 else down, False)

    def places(owner):
        hot = (lax.broadcasted_iota(jnp.int32, (16, TOK), 0) == owner).astype(F32)
        order = lax.broadcasted_iota(jnp.int32, (TOK, TOK), 0) <= lax.broadcasted_iota(jnp.int32, (TOK, TOK), 1)
        count = dot(hot.astype(BF), order.astype(F32).astype(BF), ((1,), (0,)))
        rank = jnp.sum(count * hot, axis=0, keepdims=True) - 1.0
        return owner * SLOTS + rank.astype(jnp.int32)

    slot = [places(own_ref[...]), None]

    @pl.when(near)
    def _():
        weights(1)

    got(vg.at[0, top, cols(left)], x_r.at[0])
    send(vg.at[0, top, cols(left)], vg.at[0, top, cols(left)], x_s.at[4], x_r.at[4], at(x_=right))
    send(vg.at[0, top, cols(left)], vg.at[1, top, cols(left)], v_s.at[1], v_r.at[1], partner)
    got(vg.at[0, low, cols(right)], x_r.at[2])
    send(vg.at[0, low, cols(right)], vg.at[0, low, cols(right)], x_s.at[5], x_r.at[5], at(x_=left))
    send(vg.at[0, low, cols(right)], vg.at[1, low, cols(right)], v_s.at[2], v_r.at[2], partner)

    @pl.when(near)
    def _():
        weights(2)

    def weight_tile(q):
        total = None
        for b in range(2):
            part = dot(li2[b], vg[b, :, cols(q)], ((0,), (0,))).astype(BF).astype(F32)
            total = part if total is None else total + part
        total = total.astype(BF)
        wp[2 * q] = total[:, :COLS]
        wp[2 * q + 1] = total[:, COLS:]

    own_vg.wait()
    own_li.wait()
    got(li2.at[1], p_r.at[0])
    got(vg.at[1, :, cols(x)], v_r.at[0])
    weight_tile(x)

    @pl.when(near)
    def _():
        weights(3)

    got(vg.at[0, low, cols(left)], x_r.at[1])
    send(vg.at[0, low, cols(left)], vg.at[1, low, cols(left)], v_s.at[3], v_r.at[3], partner)
    got(vg.at[0, top, cols(right)], x_r.at[3])
    send(vg.at[0, top, cols(right)], vg.at[1, top, cols(right)], v_s.at[4], v_r.at[4], partner)

    @pl.when(near)
    def _():
        weights(4)

    got(own_p, p_r.at[1])
    got(key_p, p_r.at[2])
    slot[1] = places(own_p[...])
    own_res.wait()
    got(res2.at[1], p_r.at[3])
    for h in range(2):
        acc[h] = res2[:, :, h * PART : (h + 1) * PART].astype(F32)

    @pl.when(near)
    def _():
        pltpu.make_async_copy(wsh_ref, w.at[block(y)], loc.at[3]).wait()

    @pl.when(far)
    def _():
        got(w.at[half(y, 0)], wz_r.at[0])
        got(w.at[half(y, 1)], wz_r.at[8])
        for k in range(1, 4):
            for h in range(2):
                got(w.at[half((y + NY - k) % NY, h)], wz_r.at[8 + 2 * k - 1 + h])
                got(w.at[half((y + k) % NY, h)], wz_r.at[2 * k - 1 + h])
        got(w.at[half((y + 4) % NY, 0)], wz_r.at[7])
        got(w.at[half((y + 4) % NY, 1)], wz_r.at[15])

    def back_tile(q, h):
        for b in range(2):
            acc[h, b] += dot(vg[b, :, cols(q)], w[h * PART : (h + 1) * PART, cols(q)], ((1,), (1,)))

    back_tile(x, 0)
    back_tile(x, 1)
    got(vg.at[1, top, cols(left)], v_r.at[1])
    got(vg.at[1, low, cols(left)], v_r.at[3])
    back_tile(left, 0)
    back_tile(left, 1)

    across = (x + 2) % NX
    got(vg.at[0, top, cols(across)], x_r.at[4])
    send(vg.at[0, top, cols(across)], vg.at[1, top, cols(across)], v_s.at[5], v_r.at[5], partner)
    got(vg.at[0, low, cols(across)], x_r.at[5])
    send(vg.at[0, low, cols(across)], vg.at[1, low, cols(across)], v_s.at[6], v_r.at[6], partner)

    got(vg.at[1, low, cols(right)], v_r.at[2])
    got(vg.at[1, top, cols(right)], v_r.at[4])
    back_tile(right, 0)
    back_tile(right, 1)
    got(vg.at[1, top, cols(across)], v_r.at[5])
    got(vg.at[1, low, cols(across)], v_r.at[6])

    line = lax.broadcasted_iota(jnp.int32, (2 * SLOTS, 1), 0)
    keys = [jnp.broadcast_to((ref[...] + 1).astype(F32), (8, TOK)).astype(BF) for ref in (key_ref, key_p)]

    def pack(d, h):
        to = (y + d) % NY
        wanted = (line // SLOTS) * (NY * SLOTS) + to * SLOTS + line % SLOTS
        for b in range(2):
            pick = (wanted == slot[b]).astype(F32).astype(BF)
            pk[h, d, pl.ds(b * 2 * SLOTS, 2 * SLOTS)] = dot(pick, igb[h, b], ((1,), (0,))).astype(BF)
            if h == 0:
                km[d, :, pl.ds(b * 2 * SLOTS, 2 * SLOTS)] = dot(keys[b], pick, ((1,), (1,)))
        if d > 0:
            if h == 0:
                send(km.at[d], kmr.at[d], m_s.at[d], m_r.at[d], at(y_=to))
            send(pk.at[h, d], kr.at[h, d], k_s.at[8 * h + d], k_r.at[8 * h + d], at(y_=to))

    for h in range(2):
        back_tile(across, h)
        igb[h] = acc[h].astype(BF)
        for d in (*ORDER, 0):
            pack(d, h)

    weight_tile(left)
    weight_tile(right)
    weight_tile(across)

    def rows(r):
        return pl.ds(r * PART, PART)

    def hop(way, s, r, src, dst):
        number = 8 * way + 2 * s + r
        send(src, dst, c_s.at[number], c_r.at[number], up if way == 0 else down)

    def goal(way, s):
        return (z + 4 - s) % NZ if way == 0 else (z + 4 + s) % NZ

    for way in range(2):
        hop(way, 0, way, wp.at[goal(way, 0), rows(way)], cr.at[way, 0, rows(way)])
    for way in range(2):
        hop(way, 1, 1 - way, wp.at[goal(way, 1), rows(1 - way)], cr.at[way, 1, rows(1 - way)])
    for s in range(1, 4):
        for turn in range(2):
            for way in range(2):
                r = 1 - way if turn == 0 else way
                if s == 1 and r != way:
                    continue
                got(cr.at[way, s - 1, rows(r)], c_r.at[8 * way + 2 * (s - 1) + r])
                total = wp[goal(way, s), rows(r)].astype(F32) + cr[way, s - 1, rows(r)].astype(F32)
                if s < 3:
                    cs[way, s - 1, rows(r)] = total.astype(BF)
                    hop(way, s, r, cs.at[way, s - 1, rows(r)], cr.at[way, s, rows(r)])
                else:
                    cfs[way, rows(r)] = total
                    hop(way, s, r, cfs.at[way, rows(r)], cfr.at[way, rows(r)])

    lane = lax.broadcasted_iota(jnp.int32, (1, 4 * SLOTS), 1)
    offset = ((lane // SLOTS) % 2) * KEYS - 1

    def tally(rows_, marks):
        named = marks[0:1, :].astype(jnp.int32)
        number = jnp.where(named > 0, named + offset, -1)
        hit = (lax.broadcasted_iota(jnp.int32, (2 * KEYS, 4 * SLOTS), 0) == number).astype(F32).astype(BF)
        return dot(hit, rows_, ((1,), (0,)))

    def piece(place):
        return block((place % 2) * NH + place // 2)

    def tables(h):
        table[h] = tally(pk[h, 0], km[0])
        for d in ORDER:
            if h == 0:
                got(kmr.at[d], m_r.at[d])
            got(kr.at[h, d], k_r.at[8 * h + d])
            table[h] += tally(kr[h, d], kmr[d])
        tb[h] = table[h].astype(BF)
        for d in ORDER:
            to = (z + d) % NZ
            send(tb.at[h, piece(to)], zr.at[h, d], z_s.at[8 * h + d], z_r.at[8 * h + d], at(z_=to))

    def strip(i, h):
        return pl.ds(pl.multiple_of(i * FEAT + h * PART, PART), PART)

    def finish_keys(h):
        total = table[h, piece(z), :]
        for d in ORDER:
            got(zr.at[h, d], z_r.at[8 * h + d])
            total = total + zr[h, d].astype(F32)
        kb[h] = total.astype(BF)
        here = kout.at[block(zh), strip(c, h)]
        for e in (2, 1, 3):
            send(kb.at[h], here, d_s.at[4 * h + e], d_r.at[4 * h + e], at(z_=((zh + e) % NH) * 2 + zl))
        send(kb.at[h], here, e_s.at[4 * h], e_r.at[4 * h], partner)
        pltpu.make_async_copy(kb.at[h], here, loc.at[4 + h]).start()

    def pass_keys(h):
        for e in (1, 3, 2):
            here = kout.at[block((zh + NH - e) % NH), strip(c, h)]
            got(here, d_r.at[4 * h + e])
            send(here, here, e_s.at[4 * h + e], e_r.at[4 * h + e], partner)

    for r in range(2):
        for way in range(2):
            got(cfr.at[way, rows(r)], c_r.at[8 * way + 6 + r])
        total = wp[z, rows(r)].astype(F32) + cfr[0, rows(r)] + cfr[1, rows(r)]
        ctot[rows(r)] = total
        ws[rows(r)] = total.astype(BF)
    for d in ORDER:
        to = (y + d) % NY
        send(ws.at[block(to)], yr.at[d], b_s.at[d], b_r.at[d], at(y_=to))

    tables(0)
    finish_keys(0)
    pass_keys(0)
    tables(1)

    total = ctot[block(y), :]
    for d in ORDER:
        got(yr.at[d], b_r.at[d])
        total = total + yr[d].astype(F32)
    wf[...] = total

    def heads(i):
        return pl.ds(pl.multiple_of(i * COLS, COLS), COLS)

    for e in (2, 1, 3):
        send(wf, wout.at[:, heads(z)], f_s.at[e], f_r.at[z], at(z_=((zh + e) % NH) * 2 + c))

    @pl.when(far)
    def _():
        send(wf, wout.at[:, heads(z)], f_s.at[0], f_r.at[z], at(z_=zh * 2 + c), False)

    @pl.when(near)
    def _():
        pltpu.make_async_copy(wf, wout.at[:, heads(z)], loc.at[6]).start()
        send(wf, wout.at[:, heads(z)], g_s.at[0], g_r.at[0], partner, False)

    finish_keys(1)

    @pl.when(near)
    def _():
        for d in (1, 7, 2, 6, 3, 5, 4):
            here = wout.at[:, heads((z + d) % NZ)]
            got(here, f_r.at[(z + d) % NZ])
            send(here, here, g_s.at[d], g_r.at[d], partner, False)

    pass_keys(1)

    @pl.when(far)
    def _():
        for d in range(NZ):
            got(wout.at[:, heads((z + d) % NZ)], g_r.at[d])

    for h in range(2):
        for e in range(NH):
            got(kout.at[block((zh + NH - e) % NH), strip(1 - c, h)], e_r.at[4 * h + e])
        got(kb.at[h], loc.at[4 + h])

    for src, sem in ended:
        got(src, sem)

    @pl.when(near)
    def _():
        for number in (0, 1, 2, 3, 4, 5, 6, 8, 9, 10, 11, 12, 13, 15):
            got(wsh_ref.at[first], wy_s.at[number])
        for number in range(16):
            got(wsh_ref.at[first], wz_s.at[number])
        for d in range(NZ):
            got(wf, g_s.at[d])
        got(wf, loc.at[6])

    @pl.when(far)
    def _():
        got(wf, f_s.at[0])


def body(layer_input, value_grad, residual_grad, value_weight, owner, key_row):
    dma = pltpu.SemaphoreType.DMA
    vmem = pl.BlockSpec(memory_space=pltpu.VMEM)
    hbm = pl.BlockSpec(memory_space=pl.ANY)
    scratch = [
        pltpu.VMEM((2, TOK, WIDTH), BF),
        pltpu.VMEM((2, TOK, FEAT), BF),
        pltpu.VMEM((2, TOK, FEAT), BF),
        pltpu.VMEM((1, TOK), jnp.int32),
        pltpu.VMEM((1, TOK), jnp.int32),
        pltpu.VMEM((FEAT, WIDTH), BF),
        pltpu.VMEM((NZ, FEAT, COLS), BF),
        pltpu.VMEM((2, 3, FEAT, COLS), BF),
        pltpu.VMEM((2, 2, FEAT, COLS), BF),
        pltpu.VMEM((2, FEAT, COLS), F32),
        pltpu.VMEM((2, FEAT, COLS), F32),
        pltpu.VMEM((FEAT, COLS), F32),
        pltpu.VMEM((FEAT, COLS), BF),
        pltpu.VMEM((NY, ROWS, COLS), BF),
        pltpu.VMEM((ROWS, COLS), F32),
        pltpu.VMEM((2, 2, TOK, PART), F32),
        pltpu.VMEM((2, 2, TOK, PART), BF),
        pltpu.VMEM((2, NY, 4 * SLOTS, PART), BF),
        pltpu.VMEM((NY, 8, 4 * SLOTS), F32),
        pltpu.VMEM((2, NY, 4 * SLOTS, PART), BF),
        pltpu.VMEM((NY, 8, 4 * SLOTS), F32),
        pltpu.VMEM((2, 2 * KEYS, PART), F32),
        pltpu.VMEM((2, 2 * KEYS, PART), BF),
        pltpu.VMEM((2, NZ, ROWS, PART), BF),
        pltpu.VMEM((2, ROWS, PART), BF),
        dma((7,)),
    ]
    for number in (4, 6, 7, 16, 16, 16, 16, 8, 8, 16, 8, 8):
        scratch += [dma((number,)), dma((number,))]
    scratch += [dma((4,)), dma((8,)), dma((8,)), dma((8,))]
    weight_grad, key_grad = pl.pallas_call(
        kernel,
        out_shape=(
            jax.ShapeDtypeStruct((ROWS, WIDTH), F32),
            jax.ShapeDtypeStruct((KEYS, 2 * FEAT), BF),
        ),
        in_specs=[hbm, hbm, hbm, hbm, vmem, vmem],
        out_specs=(hbm, hbm),
        scratch_shapes=scratch,
        compiler_params=pltpu.CompilerParams(
            collective_id=0, has_side_effects=True, vmem_limit_bytes=60 * 1024 * 1024
        ),
    )(layer_input, value_grad, residual_grad, value_weight, owner.reshape(1, TOK), key_row.reshape(1, TOK))
    return weight_grad, key_grad.astype(F32)


def solution(mesh):
    return jax.shard_map(
        body,
        mesh=mesh,
        in_specs=(
            P(("dp", "fsdp"), "tp"),
            P(("dp", "fsdp"), "tp"),
            P(("dp", "fsdp"), "tp"),
            P(("tp", "fsdp"), None),
            P(("dp", "fsdp"), None),
            P(("dp", "fsdp")),
        ),
        out_specs=(P(("tp", "fsdp"), None), P("fsdp", "tp")),
        check_vma=False,
    )
```

time: 131 us -> 115 us (0.88)
  Pallas kernels: 127 us -> 111 us
  other arithmetic: 0 us -> 2.18 us
  local copies, waits for them, and re-layouts: 2.93 us -> 0.8 us
    pallas_call x1, Pallas kernels: 127 us -> 111 us  [body(): pl.pallas_call(kernel, out_shape=(jax.ShapeDtypeStruct((ROWS, WIDTH), F32...]
    convert_element_type x0 -> x1, other arithmetic: none -> 2.18 us  [body(): return (weight_grad, key_grad.astype(F32))]
    unnamed x4 -> x3, local copies, waits for them, and re-layouts: 2.93 us -> 0.8 us
where the time goes in v2:
time: 115 us
  Pallas kernels  111 us (97%)
  other arithmetic  2.18 us (2%)
    pallas_call x1, Pallas kernels, body(): pl.pallas_call(kernel, out_shape=(jax.ShapeDtypeStruct((ROWS, WIDTH), F32...  111 us

profile of v2, /device:TPU:1, one launch (start us, length us, event | category | flops | bytes accessed | tf_op | source)
XLA Modules:
  0.0 114.5 jit_solution(14306623105826751966)
XLA Ops:
  0.6 110.9 %shard_map.77 = (f32[64,2048]{1,0:T(8,128)}, bf16[256,1024]{1,0:T(8,128)(2,1)}) custom-call(bf16[512,1024]{1,0:T(8,128)(2,1)} %li_ref.1, bf16[512,512]{1,0:T(8,128)(2,1)} %vgr_ref.1, bf16[512,1024]{1,0:T(8,128)(2,1)} %res_ref.1, bf16[64,2048]{1,0:T(8,128)(2,1)} %wsh_ref.1, s32[1,512]{1,0:T(1,128)} %bitcast.2, s32[1,512]{1,0:T(1,128)} %bitcast.3), custom_call_target="tpu_custom_call" | custom-call | tf_op jit(solution)/shard_map/pallas_call | solution.py:432
  111.5 0.0 copy-start
  111.5 2.2 %convert_element_type.3 = f32[256,1024]{1,0:T(8,128)} convert(bf16[256,1024]{1,0:T(8,128)(2,1)} %get-tuple-element.5) | non-fusion elementwise | flops 262144 | bytes 1572864 | tf_op jit(solution)/shard_map/convert_element_type | solution.py:445
  113.7 0.0 copy-done
  113.7 0.8 copy.9
Async XLA Ops:
  111.5 2.2 %copy-start = (f32[64,2048]{1,0:T(8,128)S(1)}, f32[64,2048]{1,0:T(8,128)}, u32[]{:S(2)}) copy-start(f32[64,2048]{1,0:T(8,128)} %get-tuple-element.8) | copy-start | bytes 1572868

commit v3 on v2

v3 whole, which is shorter than its diff:
```python
import jax
import jax.numpy as jnp
from jax import lax
from jax.experimental import pallas as pl
from jax.experimental.pallas import tpu as pltpu
from jax.sharding import PartitionSpec as P

MESH = pl.DeviceIdType.MESH
BF, F32 = jnp.bfloat16, jnp.float32
NX, NY, NZ, NH = 4, 8, 8, 4
TOK, FEAT, HEADS, WIDTH = 512, 512, 512, 2048
SLOTS, KEYS, ROWS, COLS = 64, 256, 64, 256
HALF = TOK // 2
PART = FEAT // 2
ORDER = (4, 3, 5, 2, 6, 1, 7)
CHUNKS = ((0, 256), (256, 128), (384, 128))
REST = pl.ds(1, NY - 1)


def dot(a, b, dims):
    return lax.dot_general(a, b, (dims, ((), ())), preferred_element_type=F32)


def kernel(
    li_ref, vgr_ref, res_ref, wsh_ref, own_ref, key_ref,
    wout, kout,
    vg, li2, res2, own_p, key_p, w, wp, cr, cs, cfs, cfr, ctot, ws, yr, wf, acc, igb, pk0, pk1, pk2, km, kr0, kr1, kr2, kmr, table, tb0, tb1, tb2, zr0, zr1, zr2, kb0, kb1, kb2,
    loc, p_s, p_r, x_s, x_r, v_s, v_r, wy_s, wy_r, wz_s, wz_r,
    c_s, c_r, k_s, k_r, m_s, m_r, b_s, b_r, z_s, z_r, d_s, d_r, e_s, e_r, f_s, f_r, g_s, g_r,
):
    dp, fs, x = lax.axis_index("dp"), lax.axis_index("fsdp"), lax.axis_index("tp")
    zh, c, zl, y = dp // 2, dp % 2, fs // NY, fs % NY
    z = zh * 2 + zl
    near = zl == c
    far = zl != c

    def at(x_=x, y_=y, z_=z, c_=c):
        return ((z_ // 2) * 2 + c_, (z_ % 2) * NY + y_, x_)

    partner = at(c_=1 - c)
    right, left = (x + 1) % NX, (x + NX - 1) % NX
    pk, kr, tb = (pk0, pk1, pk2), (kr0, kr1, kr2), (tb0, tb1, tb2)
    zr, kb = (zr0, zr1, zr2), (kb0, kb1, kb2)

    def send(src, dst, ss, rs, to):
        pltpu.make_async_remote_copy(
            src_ref=src, dst_ref=dst, send_sem=ss, recv_sem=rs, device_id=to, device_id_type=MESH
        ).start()

    def got(dst, rs):
        pltpu.make_async_copy(dst, dst, rs).wait()

    def cols(i):
        return pl.ds(pl.multiple_of(i * HEADS, HEADS), HEADS)

    def mine(i):
        return pl.ds(pl.multiple_of(i * FEAT, FEAT), FEAT)

    def half(i, h):
        return pl.ds(pl.multiple_of(i * ROWS + h * 32, 32), 32)

    def block(i):
        return pl.ds(pl.multiple_of(i * ROWS, ROWS), ROWS)

    barrier = pltpu.get_barrier_semaphore()
    peers = [partner, at(x_=right), at(x_=left)]
    peers += [at(y_=(y + d) % NY) for d in range(1, NY)] + [at(z_=(z + d) % NZ) for d in range(1, NZ)]
    for peer in peers:
        pl.semaphore_signal(barrier, inc=1, device_id=peer, device_id_type=MESH)

    own_vg = pltpu.make_async_copy(vgr_ref, vg.at[0, :, cols(x)], loc.at[0])
    own_vg.start()
    own_li = pltpu.make_async_copy(li_ref.at[:, mine(c)], li2.at[0], loc.at[1])
    own_li.start()
    own_res = pltpu.make_async_copy(res_ref.at[:, mine(c)], res2.at[0], loc.at[2])
    own_res.start()

    @pl.when(near)
    def _():
        pltpu.make_async_copy(wsh_ref, w.at[block(y)], loc.at[3]).start()

    pl.semaphore_wait(barrier, len(peers))

    up, down = at(z_=(z + 1) % NZ), at(z_=(z + NZ - 1) % NZ)
    after, before = at(y_=(y + 1) % NY), at(y_=(y + NY - 1) % NY)
    first, second = pl.ds(0, 32), pl.ds(32, 32)

    @pl.when(near)
    def _():
        for h, rows in enumerate((first, second)):
            send(wsh_ref.at[rows], w.at[half(y, h)], wy_s.at[0], wy_r.at[h], after)
            send(wsh_ref.at[rows], w.at[half(y, h)], wy_s.at[0], wy_r.at[8 + h], before)
        send(wsh_ref.at[first], w.at[half(y, 0)], wz_s.at[0], wz_r.at[0], up)
        send(wsh_ref.at[second], w.at[half(y, 1)], wz_s.at[0], wz_r.at[0], down)

    top, low = pl.ds(0, HALF), pl.ds(HALF, HALF)
    send(vgr_ref.at[top], vg.at[0, top, cols(x)], x_s.at[0], x_r.at[0], at(x_=right))
    send(vgr_ref.at[low], vg.at[0, low, cols(x)], x_s.at[0], x_r.at[2], at(x_=left))
    send(vgr_ref.at[low], vg.at[0, low, cols(x)], x_s.at[0], x_r.at[1], at(x_=right))
    send(vgr_ref.at[top], vg.at[0, top, cols(x)], x_s.at[0], x_r.at[3], at(x_=left))
    send(vgr_ref, vg.at[1, :, cols(x)], v_s.at[0], v_r.at[0], partner)
    send(li_ref.at[:, mine(1 - c)], li2.at[1], p_s.at[0], p_r.at[0], partner)
    send(own_ref, own_p, p_s.at[1], p_r.at[1], partner)
    send(key_ref, key_p, p_s.at[2], p_r.at[2], partner)
    send(res_ref.at[:, mine(1 - c)], res2.at[1], p_s.at[0], p_r.at[3], partner)

    def weights(k):
        plus, minus = (y + NY - k) % NY, (y + k) % NY
        for h in range(2):
            for base, shard, onward, side, keeps in ((0, plus, after, down, 0), (8, minus, before, up, 1)):
                if k == 4 and h != keeps:
                    continue
                here = w.at[half(shard, h)]
                got(here, wy_r.at[base + 2 * (k - 1) + h])
                if k < 3 or (k == 3 and h == keeps):
                    send(here, here, wy_s.at[0], wy_r.at[base + 2 * k + h], onward)
                if k < 4:
                    send(here, here, wz_s.at[0], wz_r.at[0], side)
                else:
                    send(here, here, wz_s.at[0], wz_r.at[0], up if base == 0 else down)

    def places(owner):
        hot = (lax.broadcasted_iota(jnp.int32, (16, TOK), 0) == owner).astype(F32)
        order = lax.broadcasted_iota(jnp.int32, (TOK, TOK), 0) <= lax.broadcasted_iota(jnp.int32, (TOK, TOK), 1)
        count = dot(hot.astype(BF), order.astype(F32).astype(BF), ((1,), (0,)))
        rank = jnp.sum(count * hot, axis=0, keepdims=True) - 1.0
        return owner * SLOTS + rank.astype(jnp.int32)

    slot = [places(own_ref[...]), None]

    @pl.when(near)
    def _():
        weights(1)

    got(vg.at[0, top, cols(left)], x_r.at[0])
    send(vg.at[0, top, cols(left)], vg.at[0, top, cols(left)], x_s.at[0], x_r.at[4], at(x_=right))
    send(vg.at[0, top, cols(left)], vg.at[1, top, cols(left)], v_s.at[0], v_r.at[1], partner)
    got(vg.at[0, low, cols(right)], x_r.at[2])
    send(vg.at[0, low, cols(right)], vg.at[0, low, cols(right)], x_s.at[0], x_r.at[5], at(x_=left))
    send(vg.at[0, low, cols(right)], vg.at[1, low, cols(right)], v_s.at[0], v_r.at[2], partner)

    @pl.when(near)
    def _():
        weights(2)

    def weight_tile(q):
        total = None
        for b in range(2):
            part = dot(li2[b], vg[b, :, cols(q)], ((0,), (0,))).astype(BF).astype(F32)
            total = part if total is None else total + part
        wp[2 * q] = total[:, :COLS]
        wp[2 * q + 1] = total[:, COLS:]

    own_vg.wait()
    own_li.wait()
    got(li2.at[1], p_r.at[0])
    got(vg.at[1, :, cols(x)], v_r.at[0])
    weight_tile(x)

    got(own_p, p_r.at[1])
    got(key_p, p_r.at[2])
    slot[1] = places(own_p[...])
    own_res.wait()
    got(res2.at[1], p_r.at[3])
    acc[...] = res2[...].astype(F32)

    got(vg.at[0, low, cols(left)], x_r.at[1])
    send(vg.at[0, low, cols(left)], vg.at[1, low, cols(left)], v_s.at[0], v_r.at[1], partner)
    got(vg.at[0, top, cols(right)], x_r.at[3])
    send(vg.at[0, top, cols(right)], vg.at[1, top, cols(right)], v_s.at[0], v_r.at[2], partner)

    @pl.when(near)
    def _():
        weights(3)

    got(vg.at[1, :, cols(left)], v_r.at[1])
    weight_tile(left)
    got(vg.at[1, :, cols(right)], v_r.at[2])
    weight_tile(right)

    @pl.when(near)
    def _():
        weights(4)

    across = (x + 2) % NX
    got(vg.at[0, top, cols(across)], x_r.at[4])
    send(vg.at[0, top, cols(across)], vg.at[1, top, cols(across)], v_s.at[0], v_r.at[3], partner)
    got(vg.at[0, low, cols(across)], x_r.at[5])
    send(vg.at[0, low, cols(across)], vg.at[1, low, cols(across)], v_s.at[0], v_r.at[3], partner)

    @pl.when(near)
    def _():
        pltpu.make_async_copy(wsh_ref, w.at[block(y)], loc.at[3]).wait()

    @pl.when(far)
    def _():
        got(w, wz_r.at[0])

    def back_tile(q, h=None):
        start, size = (0, FEAT) if h is None else CHUNKS[h]
        for b in range(2):
            acc[b, :, start : start + size] += dot(vg[b, :, cols(q)], w[start : start + size, cols(q)], ((1,), (1,)))

    back_tile(x)
    back_tile(left)
    back_tile(right)
    got(vg.at[1, :, cols(across)], v_r.at[3])

    line = lax.broadcasted_iota(jnp.int32, (2 * SLOTS, 1), 0)
    keys = [jnp.broadcast_to((ref[...] + 1).astype(F32), (8, TOK)).astype(BF) for ref in (key_ref, key_p)]

    def pack(h):
        start, size = CHUNKS[h]
        back_tile(across, h)
        igb[:, :, start : start + size] = acc[:, :, start : start + size].astype(BF)
        for d in (*ORDER, 0):
            to = (y + d) % NY
            wanted = (line // SLOTS) * (NY * SLOTS) + to * SLOTS + line % SLOTS
            for b in range(2):
                pick = (wanted == slot[b]).astype(F32).astype(BF)
                picked = dot(pick, igb[b, :, start : start + size], ((1,), (0,)))
                pk[h][d, pl.ds(b * 2 * SLOTS, 2 * SLOTS)] = picked.astype(BF)
                if h == 0:
                    km[d, :, pl.ds(b * 2 * SLOTS, 2 * SLOTS)] = dot(keys[b], pick, ((1,), (1,)))
            if h < 2 and d > 0:
                ship(h, d)

    def ship(h, d):
        to = at(y_=(y + d) % NY)
        if h == 0:
            send(km.at[d], kmr.at[d], m_s.at[0], m_r.at[0], to)
        send(pk[h].at[d], kr[h].at[d], k_s.at[h], k_r.at[8 * h + d], to)

    def rows(r):
        return pl.ds(r * PART, PART)

    def hop(way, s, r, src, dst):
        number = 8 * way + 2 * s + r
        send(src, dst, c_s.at[0], c_r.at[number], up if way == 0 else down)

    def goal(way, s):
        return (z + 4 - s) % NZ if way == 0 else (z + 4 + s) % NZ

    def start(way, s, r):
        cs[way, s, rows(r)] = wp[goal(way, s), rows(r)].astype(BF)
        hop(way, s, r, cs.at[way, s, rows(r)], cr.at[way, s, rows(r)])

    pack(0)
    weight_tile(across)
    for way in range(2):
        start(way, 0, way)
    for way in range(2):
        start(way, 1, 1 - way)
    pack(1)
    for s in range(1, 4):
        if s == 2:
            pack(2)
        for turn in range(2):
            for way in range(2):
                r = 1 - way if turn == 0 else way
                if s == 1 and r != way:
                    continue
                got(cr.at[way, s - 1, rows(r)], c_r.at[8 * way + 2 * (s - 1) + r])
                total = wp[goal(way, s), rows(r)] + cr[way, s - 1, rows(r)].astype(F32)
                if s < 3:
                    cs[way, s, rows(r)] = total.astype(BF)
                    hop(way, s, r, cs.at[way, s, rows(r)], cr.at[way, s, rows(r)])
                else:
                    cfs[way, rows(r)] = total
                    hop(way, s, r, cfs.at[way, rows(r)], cfr.at[way, rows(r)])

    lane = lax.broadcasted_iota(jnp.int32, (1, 4 * SLOTS), 1)
    offset = ((lane // SLOTS) % 2) * KEYS - 1

    def tally(rows_, marks):
        named = marks[0:1, :].astype(jnp.int32)
        number = jnp.where(named > 0, named + offset, -1)
        hit = (lax.broadcasted_iota(jnp.int32, (2 * KEYS, 4 * SLOTS), 0) == number).astype(F32).astype(BF)
        return dot(hit, rows_, ((1,), (0,)))

    def piece(place):
        return block((place % 2) * NH + place // 2)

    def tables(h):
        start, size = CHUNKS[h]
        here = pl.ds(start, size)
        if h == 0:
            got(kmr.at[REST], m_r.at[0])
        table[:, here] = tally(pk[h][0], km[0])
        for d in ORDER:
            got(kr[h].at[d], k_r.at[8 * h + d])
            table[:, here] += tally(kr[h][d], kmr[d])
        tb[h][...] = table[:, here].astype(BF)
        for d in ORDER:
            to = (z + d) % NZ
            send(tb[h].at[piece(to)], zr[h].at[d], z_s.at[h], z_r.at[h], at(z_=to))

    def strip(i, h):
        start, size = CHUNKS[h]
        return pl.ds(pl.multiple_of(i * FEAT + start, 128), size)

    def finish_keys(h):
        start, size = CHUNKS[h]
        got(zr[h].at[REST], z_r.at[h])
        total = table[piece(z), pl.ds(start, size)]
        for d in ORDER:
            total = total + zr[h][d].astype(F32)
        kb[h][...] = total.astype(BF)
        here = kout.at[block(zh), strip(c, h)]
        for e in (2, 1, 3):
            send(kb[h], here, d_s.at[0], d_r.at[4 * h + e], at(z_=((zh + e) % NH) * 2 + zl))
        send(kb[h], here, e_s.at[0], e_r.at[0], partner)
        pltpu.make_async_copy(kb[h], here, loc.at[4 + h]).start()

    def pass_keys(h):
        for e in (1, 3, 2):
            here = kout.at[block((zh + NH - e) % NH), strip(c, h)]
            got(here, d_r.at[4 * h + e])
            send(here, here, e_s.at[0], e_r.at[0], partner)

    tables(0)

    for r in range(2):
        for way in range(2):
            got(cfr.at[way, rows(r)], c_r.at[8 * way + 6 + r])
        total = wp[z, rows(r)] + cfr[0, rows(r)] + cfr[1, rows(r)]
        ctot[rows(r)] = total
        ws[rows(r)] = total.astype(BF)
    for d in ORDER:
        to = (y + d) % NY
        send(ws.at[block(to)], yr.at[d], b_s.at[0], b_r.at[0], at(y_=to))
    for d in ORDER:
        ship(2, d)

    tables(1)
    finish_keys(0)

    got(yr.at[REST], b_r.at[0])
    total = ctot[block(y), :]
    for d in ORDER:
        total = total + yr[d].astype(F32)
    wf[...] = total

    def heads(i):
        return pl.ds(pl.multiple_of(i * COLS, COLS), COLS)

    for e in (2, 1, 3):
        send(wf, wout.at[:, heads(z)], f_s.at[0], f_r.at[z], at(z_=((zh + e) % NH) * 2 + c))

    @pl.when(far)
    def _():
        send(wf, wout.at[:, heads(z)], f_s.at[0], f_r.at[z], at(z_=zh * 2 + c))

    @pl.when(near)
    def _():
        pltpu.make_async_copy(wf, wout.at[:, heads(z)], loc.at[7]).start()
        send(wf, wout.at[:, heads(z)], g_s.at[0], g_r.at[0], partner)

    finish_keys(1)
    pass_keys(0)
    tables(2)
    pass_keys(1)

    @pl.when(near)
    def _():
        for d in (1, 7, 2, 6, 3, 5, 4):
            here = wout.at[:, heads((z + d) % NZ)]
            got(here, f_r.at[(z + d) % NZ])
            send(here, here, g_s.at[0], g_r.at[0], partner)

    finish_keys(2)
    pass_keys(2)

    @pl.when(far)
    def _():
        got(wout, g_r.at[0])

    got(kout.at[:, mine(1 - c)], e_r.at[0])
    for h in range(3):
        got(kb[h], loc.at[4 + h])

    got(vg.at[0, :, pl.ds(0, 3 * HEADS)], x_s.at[0])
    got(vg.at[0], v_s.at[0])
    got(li2, p_s.at[0])
    got(own_p, p_s.at[1])
    got(key_p, p_s.at[2])
    got(vg.at[:, pl.ds(0, 288)], c_s.at[0])
    for h in range(3):
        got(kr[h].at[REST], k_s.at[h])
        got(zr[h].at[REST], z_s.at[h])
    got(kmr.at[REST], m_s.at[0])
    got(yr.at[REST], b_s.at[0])
    got(w.at[pl.ds(0, 48)], d_s.at[0])
    got(w.at[pl.ds(0, 64)], e_s.at[0])

    @pl.when(near)
    def _():
        got(w.at[pl.ds(0, 448)], wy_s.at[0])
        got(w, wz_s.at[0])
        got(w.at[pl.ds(0, 48)], f_s.at[0])
        got(w.at[pl.ds(0, 128)], g_s.at[0])
        got(wf, loc.at[7])

    @pl.when(far)
    def _():
        got(w.at[pl.ds(0, 64)], f_s.at[0])


def body(layer_input, value_grad, residual_grad, value_weight, owner, key_row):
    dma = pltpu.SemaphoreType.DMA
    vmem = pl.BlockSpec(memory_space=pltpu.VMEM)
    hbm = pl.BlockSpec(memory_space=pl.ANY)
    scratch = [
        pltpu.VMEM((2, TOK, WIDTH), BF),
        pltpu.VMEM((2, TOK, FEAT), BF),
        pltpu.VMEM((2, TOK, FEAT), BF),
        pltpu.VMEM((1, TOK), jnp.int32),
        pltpu.VMEM((1, TOK), jnp.int32),
        pltpu.VMEM((FEAT, WIDTH), BF),
        pltpu.VMEM((NZ, FEAT, COLS), F32),
        pltpu.VMEM((2, 3, FEAT, COLS), BF),
        pltpu.VMEM((2, 3, FEAT, COLS), BF),
        pltpu.VMEM((2, FEAT, COLS), F32),
        pltpu.VMEM((2, FEAT, COLS), F32),
        pltpu.VMEM((FEAT, COLS), F32),
        pltpu.VMEM((FEAT, COLS), BF),
        pltpu.VMEM((NY, ROWS, COLS), BF),
        pltpu.VMEM((ROWS, COLS), F32),
        pltpu.VMEM((2, TOK, FEAT), F32),
        pltpu.VMEM((2, TOK, FEAT), BF),
    ]
    widths = [size for _, size in CHUNKS]
    scratch += [pltpu.VMEM((NY, 4 * SLOTS, size), BF) for size in widths]
    scratch += [pltpu.VMEM((NY, 8, 4 * SLOTS), F32)]
    scratch += [pltpu.VMEM((NY, 4 * SLOTS, size), BF) for size in widths]
    scratch += [pltpu.VMEM((NY, 8, 4 * SLOTS), F32), pltpu.VMEM((2 * KEYS, FEAT), F32)]
    scratch += [pltpu.VMEM((2 * KEYS, size), BF) for size in widths]
    scratch += [pltpu.VMEM((NZ, ROWS, size), BF) for size in widths]
    scratch += [pltpu.VMEM((ROWS, size), BF) for size in widths]
    scratch += [dma((8,))]
    for sent, received in ((3, 4), (1, 6), (1, 4), (1, 16), (1, 1), (1, 16), (3, 24), (1, 1), (1, 1), (3, 3), (1, 12), (1, 1)):
        scratch += [dma((sent,)), dma((received,))]
    scratch += [dma((1,)), dma((8,)), dma((1,)), dma((1,))]
    weight_grad, key_grad = pl.pallas_call(
        kernel,
        out_shape=(
            pltpu.VMEM((ROWS, WIDTH), F32),
            pltpu.VMEM((KEYS, 2 * FEAT), BF),
        ),
        in_specs=[hbm, hbm, hbm, hbm, vmem, vmem],
        out_specs=(vmem, vmem),
        scratch_shapes=scratch,
        compiler_params=pltpu.CompilerParams(
            collective_id=0, has_side_effects=True, vmem_limit_bytes=60 * 1024 * 1024
        ),
    )(layer_input, value_grad, residual_grad, value_weight, owner.reshape(1, TOK), key_row.reshape(1, TOK))
    return weight_grad, key_grad.astype(F32)


def solution(mesh):
    return jax.shard_map(
        body,
        mesh=mesh,
        in_specs=(
            P(("dp", "fsdp"), "tp"),
            P(("dp", "fsdp"), "tp"),
            P(("dp", "fsdp"), "tp"),
            P(("tp", "fsdp"), None),
            P(("dp", "fsdp"), None),
            P(("dp", "fsdp")),
        ),
        out_specs=(P(("tp", "fsdp"), None), P("fsdp", "tp")),
        check_vma=False,
    )
```

time: 115 us -> 108 us (0.939)
  Pallas kernels: 111 us -> 106 us
    pallas_call x1, Pallas kernels: 111 us -> 106 us  [body(): pl.pallas_call(kernel, out_shape=(pltpu.VMEM((ROWS, WIDTH), F32), pltpu.V...]
where the time goes in v3:
time: 108 us
  Pallas kernels  106 us (98%)
  other arithmetic  1.08 us (1%)
    pallas_call x1, Pallas kernels, body(): pl.pallas_call(kernel, out_shape=(pltpu.VMEM((ROWS, WIDTH), F32), pltpu.V...  106 us

profile of v3, /device:TPU:1, one launch (start us, length us, event | category | flops | bytes accessed | tf_op | source)
XLA Modules:
  0.0 108.1 jit_solution(16993699438773849687)
XLA Ops:
  0.6 105.6 %shard_map.77 = (f32[64,2048]{1,0:T(8,128)S(1)}, bf16[256,1024]{1,0:T(8,128)(2,1)S(1)}) custom-call(bf16[512,1024]{1,0:T(8,128)(2,1)} %li_ref.1, bf16[512,512]{1,0:T(8,128)(2,1)} %vgr_ref.1, bf16[512,1024]{1,0:T(8,128)(2,1)} %res_ref.1, bf16[64,2048]{1,0:T(8,128)(2,1)} %wsh_ref.1, s32[1,512]{1,0:T(1,128)} %bitcast.2, s32[1,512]{1,0:T(1,128)} %bitcast.3), custom_call_target="tpu_custom_call" | custom-call | tf_op jit(solution)/shard_map/pallas_call | solution.py:444
  106.2 0.8 copy.9
  107.0 1.1 %convert_element_type.3 = f32[256,1024]{1,0:T(8,128)} convert(bf16[256,1024]{1,0:T(8,128)(2,1)S(1)} %get-tuple-element.5) | non-fusion elementwise | flops 262144 | bytes 1572864 | tf_op jit(solution)/shard_map/convert_element_type | solution.py:457

commit v4 on v3

--- a/solution.py
+++ b/solution.py
@@ -24,9 +24,9 @@
 def kernel(
     li_ref, vgr_ref, res_ref, wsh_ref, own_ref, key_ref,
     wout, kout,
-    vg, li2, res2, own_p, key_p, w, wp, cr, cs, cfs, cfr, ctot, ws, yr, wf, acc, igb, pk0, pk1, pk2, km, kr0, kr1, kr2, kmr, table, tb0, tb1, tb2, zr0, zr1, zr2, kb0, kb1, kb2,
+    vg, li2, res2, own_p, key_p, w, wp, cr, cs, cfs, cfr, ctot, ws, yr, wf, acc, igb, pk0, pk1, pk2, km, kr0, kr1, kr2, kmr, table, tb0, tb1, tb2, zr0, zr1, zr2, kb0, kb1, kb2, gt0, gt1, gt2, gr0, gr1, gr2,
     loc, p_s, p_r, x_s, x_r, v_s, v_r, wy_s, wy_r, wz_s, wz_r,
-    c_s, c_r, k_s, k_r, m_s, m_r, b_s, b_r, z_s, z_r, d_s, d_r, e_s, e_r, f_s, f_r, g_s, g_r,
+    c_s, c_r, k_s, k_r, m_s, m_r, b_s, b_r, z_s, z_r, d_s, d_r, e_s, e_r, f_s, f_r, g_s, g_r, n_s, n_r,
 ):
     dp, fs, x = lax.axis_index("dp"), lax.axis_index("fsdp"), lax.axis_index("tp")
     zh, c, zl, y = dp // 2, dp % 2, fs // NY, fs % NY
@@ -40,7 +40,7 @@
     partner = at(c_=1 - c)
     right, left = (x + 1) % NX, (x + NX - 1) % NX
     pk, kr, tb = (pk0, pk1, pk2), (kr0, kr1, kr2), (tb0, tb1, tb2)
-    zr, kb = (zr0, zr1, zr2), (kb0, kb1, kb2)
+    zr, kb, gt, gr = (zr0, zr1, zr2), (kb0, kb1, kb2), (gt0, gt1, gt2), (gr0, gr1, gr2)
 
     def send(src, dst, ss, rs, to):
         pltpu.make_async_remote_copy(
@@ -98,11 +98,8 @@
     send(vgr_ref.at[low], vg.at[0, low, cols(x)], x_s.at[0], x_r.at[2], at(x_=left))
     send(vgr_ref.at[low], vg.at[0, low, cols(x)], x_s.at[0], x_r.at[1], at(x_=right))
     send(vgr_ref.at[top], vg.at[0, top, cols(x)], x_s.at[0], x_r.at[3], at(x_=left))
-    send(vgr_ref, vg.at[1, :, cols(x)], v_s.at[0], v_r.at[0], partner)
-    send(li_ref.at[:, mine(1 - c)], li2.at[1], p_s.at[0], p_r.at[0], partner)
     send(own_ref, own_p, p_s.at[1], p_r.at[1], partner)
     send(key_ref, key_p, p_s.at[2], p_r.at[2], partner)
-    send(res_ref.at[:, mine(1 - c)], res2.at[1], p_s.at[0], p_r.at[3], partner)
 
     def weights(k):
         plus, minus = (y + NY - k) % NY, (y + k) % NY
@@ -132,6 +129,9 @@
     def _():
         weights(1)
 
+    send(vgr_ref, vg.at[1, :, cols(x)], v_s.at[0], v_r.at[0], partner)
+    send(li_ref.at[:, mine(1 - c)], li2.at[1], p_s.at[0], p_r.at[0], partner)
+
     got(vg.at[0, top, cols(left)], x_r.at[0])
     send(vg.at[0, top, cols(left)], vg.at[0, top, cols(left)], x_s.at[0], x_r.at[4], at(x_=right))
     send(vg.at[0, top, cols(left)], vg.at[1, top, cols(left)], v_s.at[0], v_r.at[1], partner)
@@ -151,6 +151,8 @@
         wp[2 * q] = total[:, :COLS]
         wp[2 * q + 1] = total[:, COLS:]
 
+    send(res_ref.at[:, mine(1 - c)], res2.at[1], p_s.at[0], p_r.at[3], partner)
+
     own_vg.wait()
     own_li.wait()
     got(li2.at[1], p_r.at[0])
@@ -160,23 +162,14 @@
     got(own_p, p_r.at[1])
     got(key_p, p_r.at[2])
     slot[1] = places(own_p[...])
-    own_res.wait()
-    got(res2.at[1], p_r.at[3])
-    acc[...] = res2[...].astype(F32)
+    @pl.when(near)
+    def _():
+        weights(3)
 
     got(vg.at[0, low, cols(left)], x_r.at[1])
     send(vg.at[0, low, cols(left)], vg.at[1, low, cols(left)], v_s.at[0], v_r.at[1], partner)
     got(vg.at[0, top, cols(right)], x_r.at[3])
     send(vg.at[0, top, cols(right)], vg.at[1, top, cols(right)], v_s.at[0], v_r.at[2], partner)
-
-    @pl.when(near)
-    def _():
-        weights(3)
-
-    got(vg.at[1, :, cols(left)], v_r.at[1])
-    weight_tile(left)
-    got(vg.at[1, :, cols(right)], v_r.at[2])
-    weight_tile(right)
 
     @pl.when(near)
     def _():
@@ -188,6 +181,10 @@
     got(vg.at[0, low, cols(across)], x_r.at[5])
     send(vg.at[0, low, cols(across)], vg.at[1, low, cols(across)], v_s.at[0], v_r.at[3], partner)
 
+    own_res.wait()
+    got(res2.at[1], p_r.at[3])
+    acc[...] = res2[...].astype(F32)
+
     @pl.when(near)
     def _():
         pltpu.make_async_copy(wsh_ref, w.at[block(y)], loc.at[3]).wait()
@@ -202,7 +199,9 @@
             acc[b, :, start : start + size] += dot(vg[b, :, cols(q)], w[start : start + size, cols(q)], ((1,), (1,)))
 
     back_tile(x)
+    got(vg.at[1, :, cols(left)], v_r.at[1])
     back_tile(left)
+    got(vg.at[1, :, cols(right)], v_r.at[2])
     back_tile(right)
     got(vg.at[1, :, cols(across)], v_r.at[3])
 
@@ -222,14 +221,23 @@
                 pk[h][d, pl.ds(b * 2 * SLOTS, 2 * SLOTS)] = picked.astype(BF)
                 if h == 0:
                     km[d, :, pl.ds(b * 2 * SLOTS, 2 * SLOTS)] = dot(keys[b], pick, ((1,), (1,)))
-            if h < 2 and d > 0:
+            if h < 2 and 2 <= d <= 6:
                 ship(h, d)
 
+    parts = (pl.ds(0, 2 * SLOTS), pl.ds(2 * SLOTS, 2 * SLOTS))
+
     def ship(h, d):
-        to = at(y_=(y + d) % NY)
-        if h == 0:
-            send(km.at[d], kmr.at[d], m_s.at[0], m_r.at[0], to)
-        send(pk[h].at[d], kr[h].at[d], k_s.at[h], k_r.at[8 * h + d], to)
+        for way in range(2):
+            if (d, way) in ((2, 1), (3, 1), (5, 0), (6, 0)):
+                continue
+            place = d - 1 if way == 0 else d + 1
+            to = at(y_=(y + place) % NY)
+            if h == 0:
+                send(km.at[d], kmr.at[place], m_s.at[0], m_r.at[0], to)
+            src, dst = pk[h].at[d], kr[h].at[place]
+            if d == 4:
+                src, dst = pk[h].at[d, parts[way]], kr[h].at[place, parts[way]]
+            send(src, dst, k_s.at[h], k_r.at[8 * h + place], to)
 
     def rows(r):
         return pl.ds(r * PART, PART)
@@ -245,7 +253,34 @@
         cs[way, s, rows(r)] = wp[goal(way, s), rows(r)].astype(BF)
         hop(way, s, r, cs.at[way, s, rows(r)], cr.at[way, s, rows(r)])
 
+    def tally(rows_, marks):
+        slots = rows_.shape[0]
+        lane = lax.broadcasted_iota(jnp.int32, (1, slots), 1)
+        named = marks[0:1, :].astype(jnp.int32)
+        number = jnp.where(named > 0, named + ((lane // SLOTS) % 2) * KEYS - 1, -1)
+        hit = (lax.broadcasted_iota(jnp.int32, (2 * KEYS, slots), 0) == number).astype(F32).astype(BF)
+        return dot(hit, rows_, ((1,), (0,)))
+
+    def gate(h):
+        if h == 0:
+            got(kmr.at[pl.ds(0, 6)], m_r.at[0])
+        for way in range(2):
+            own, places_ = ((1, (1, 2, 3)), (7, (7, 6, 5)))[way]
+            total = tally(pk[h][own], km[own])
+            for place in places_:
+                if place in (3, 5):
+                    got(kr[h].at[place, parts[way]], k_r.at[8 * h + place])
+                    total = total + tally(kr[h][place, parts[way]], kmr[place, :, parts[way]])
+                else:
+                    got(kr[h].at[place], k_r.at[8 * h + place])
+                    total = total + tally(kr[h][place], kmr[place])
+            gt[h][way] = total.astype(BF)
+            to = after if way == 0 else before
+            send(gt[h].at[way], gr[h].at[way], n_s.at[h], n_r.at[2 * h + way], to)
+
     pack(0)
+    weight_tile(left)
+    weight_tile(right)
     weight_tile(across)
     for way in range(2):
         start(way, 0, way)
@@ -255,6 +290,10 @@
     for s in range(1, 4):
         if s == 2:
             pack(2)
+        if s == 3:
+            gate(0)
+            for d in ORDER[:5]:
+                ship(2, d)
         for turn in range(2):
             for way in range(2):
                 r = 1 - way if turn == 0 else way
@@ -269,27 +308,16 @@
                     cfs[way, rows(r)] = total
                     hop(way, s, r, cfs.at[way, rows(r)], cfr.at[way, rows(r)])
 
-    lane = lax.broadcasted_iota(jnp.int32, (1, 4 * SLOTS), 1)
-    offset = ((lane // SLOTS) % 2) * KEYS - 1
-
-    def tally(rows_, marks):
-        named = marks[0:1, :].astype(jnp.int32)
-        number = jnp.where(named > 0, named + offset, -1)
-        hit = (lax.broadcasted_iota(jnp.int32, (2 * KEYS, 4 * SLOTS), 0) == number).astype(F32).astype(BF)
-        return dot(hit, rows_, ((1,), (0,)))
-
     def piece(place):
         return block((place % 2) * NH + place // 2)
 
     def tables(h):
         start, size = CHUNKS[h]
         here = pl.ds(start, size)
-        if h == 0:
-            got(kmr.at[REST], m_r.at[0])
         table[:, here] = tally(pk[h][0], km[0])
-        for d in ORDER:
-            got(kr[h].at[d], k_r.at[8 * h + d])
-            table[:, here] += tally(kr[h][d], kmr[d])
+        for way in range(2):
+            got(gr[h].at[way], n_r.at[2 * h + way])
+            table[:, here] += gr[h][way].astype(F32)
         tb[h][...] = table[:, here].astype(BF)
         for d in ORDER:
             to = (z + d) % NZ
@@ -318,6 +346,7 @@
             got(here, d_r.at[4 * h + e])
             send(here, here, e_s.at[0], e_r.at[0], partner)
 
+    gate(1)
     tables(0)
 
     for r in range(2):
@@ -326,14 +355,17 @@
         total = wp[z, rows(r)] + cfr[0, rows(r)] + cfr[1, rows(r)]
         ctot[rows(r)] = total
         ws[rows(r)] = total.astype(BF)
+    gate(2)
     for d in ORDER:
         to = (y + d) % NY
         send(ws.at[block(to)], yr.at[d], b_s.at[0], b_r.at[0], at(y_=to))
-    for d in ORDER:
-        ship(2, d)
-
+
+    finish_keys(0)
     tables(1)
-    finish_keys(0)
+    tables(2)
+    finish_keys(1)
+    pass_keys(0)
+    finish_keys(2)
 
     got(yr.at[REST], b_r.at[0])
     total = ctot[block(y), :]
@@ -356,10 +388,8 @@
         pltpu.make_async_copy(wf, wout.at[:, heads(z)], loc.at[7]).start()
         send(wf, wout.at[:, heads(z)], g_s.at[0], g_r.at[0], partner)
 
-    finish_keys(1)
-    pass_keys(0)
-    tables(2)
     pass_keys(1)
+    pass_keys(2)
 
     @pl.when(near)
     def _():
@@ -367,9 +397,6 @@
             here = wout.at[:, heads((z + d) % NZ)]
             got(here, f_r.at[(z + d) % NZ])
             send(here, here, g_s.at[0], g_r.at[0], partner)
-
-    finish_keys(2)
-    pass_keys(2)
 
     @pl.when(far)
     def _():
@@ -386,9 +413,10 @@
     got(key_p, p_s.at[2])
     got(vg.at[:, pl.ds(0, 288)], c_s.at[0])
     for h in range(3):
-        got(kr[h].at[REST], k_s.at[h])
+        got(kr[h].at[pl.ds(0, 5)], k_s.at[h])
+        got(gr[h], n_s.at[h])
         got(zr[h].at[REST], z_s.at[h])
-    got(kmr.at[REST], m_s.at[0])
+    got(kmr.at[pl.ds(0, 6)], m_s.at[0])
     got(yr.at[REST], b_s.at[0])
     got(w.at[pl.ds(0, 48)], d_s.at[0])
     got(w.at[pl.ds(0, 64)], e_s.at[0])
@@ -437,10 +465,11 @@
     scratch += [pltpu.VMEM((2 * KEYS, size), BF) for size in widths]
     scratch += [pltpu.VMEM((NZ, ROWS, size), BF) for size in widths]
     scratch += [pltpu.VMEM((ROWS, size), BF) for size in widths]
+    scratch += [pltpu.VMEM((2, 2 * KEYS, size), BF) for size in (*widths, *widths)]
     scratch += [dma((8,))]
     for sent, received in ((3, 4), (1, 6), (1, 4), (1, 16), (1, 1), (1, 16), (3, 24), (1, 1), (1, 1), (3, 3), (1, 12), (1, 1)):
         scratch += [dma((sent,)), dma((received,))]
-    scratch += [dma((1,)), dma((8,)), dma((1,)), dma((1,))]
+    scratch += [dma((1,)), dma((8,)), dma((1,)), dma((1,)), dma((3,)), dma((6,))]
     weight_grad, key_grad = pl.pallas_call(
         kernel,
         out_shape=(

time: 108 us -> 104 us (0.963); the launches traced: 108 us -> 102 us
  Pallas kernels: 106 us -> 99.9 us
    pallas_call x1, Pallas kernels: 106 us -> 99.9 us  [body(): pl.pallas_call(kernel, out_shape=(pltpu.VMEM((ROWS, WIDTH), F32), pltpu.V...]
where the time goes in v4:
time: 104 us; the launch traced here: 102 us
  Pallas kernels  99.9 us (96%)
  other arithmetic  1.08 us (1%)
    pallas_call x1, Pallas kernels, body(): pl.pallas_call(kernel, out_shape=(pltpu.VMEM((ROWS, WIDTH), F32), pltpu.V...  99.9 us

profile of v4, /device:TPU:1, one launch (start us, length us, event | category | flops | bytes accessed | tf_op | source)
XLA Modules:
  0.0 102.4 jit_solution(6624603361929184453)
XLA Ops:
  0.6 99.9 %shard_map.77 = (f32[64,2048]{1,0:T(8,128)S(1)}, bf16[256,1024]{1,0:T(8,128)(2,1)S(1)}) custom-call(bf16[512,1024]{1,0:T(8,128)(2,1)} %li_ref.1, bf16[512,512]{1,0:T(8,128)(2,1)} %vgr_ref.1, bf16[512,1024]{1,0:T(8,128)(2,1)} %res_ref.1, bf16[64,2048]{1,0:T(8,128)(2,1)} %wsh_ref.1, s32[1,512]{1,0:T(1,128)} %bitcast.2, s32[1,512]{1,0:T(1,128)} %bitcast.3), custom_call_target="tpu_custom_call" | custom-call | tf_op jit(solution)/shard_map/pallas_call | solution.py:473
  100.5 0.8 copy.9
  101.3 1.1 %convert_element_type.3 = f32[256,1024]{1,0:T(8,128)} convert(bf16[256,1024]{1,0:T(8,128)(2,1)S(1)} %get-tuple-element.5) | non-fusion elementwise | flops 262144 | bytes 1572864 | tf_op jit(solution)/shard_map/convert_element_type | solution.py:486

commit v5 on v4

--- a/solution.py
+++ b/solution.py
@@ -363,9 +363,6 @@
     finish_keys(0)
     tables(1)
     tables(2)
-    finish_keys(1)
-    pass_keys(0)
-    finish_keys(2)
 
     got(yr.at[REST], b_r.at[0])
     total = ctot[block(y), :]
@@ -388,6 +385,9 @@
         pltpu.make_async_copy(wf, wout.at[:, heads(z)], loc.at[7]).start()
         send(wf, wout.at[:, heads(z)], g_s.at[0], g_r.at[0], partner)
 
+    finish_keys(1)
+    pass_keys(0)
+    finish_keys(2)
     pass_keys(1)
     pass_keys(2)
 

time: 104 us -> 101 us (0.971)
  Pallas kernels: 99.9 us -> 97.5 us
    pallas_call x1, Pallas kernels: 99.9 us -> 97.5 us  [body(): pl.pallas_call(kernel, out_shape=(pltpu.VMEM((ROWS, WIDTH), F32), pltpu.V...]
where the time goes in v5:
time: 101 us; the launch traced here: 100 us
  Pallas kernels  97.5 us (97%)
  other arithmetic  1.08 us (1%)
    pallas_call x1, Pallas kernels, body(): pl.pallas_call(kernel, out_shape=(pltpu.VMEM((ROWS, WIDTH), F32), pltpu.V...  97.5 us

profile of v5, /device:TPU:1, one launch (start us, length us, event | category | flops | bytes accessed | tf_op | source)
XLA Modules:
  0.0 100.0 jit_solution(5172487449502290223)
XLA Ops:
  0.6 97.5 %shard_map.77 = (f32[64,2048]{1,0:T(8,128)S(1)}, bf16[256,1024]{1,0:T(8,128)(2,1)S(1)}) custom-call(bf16[512,1024]{1,0:T(8,128)(2,1)} %li_ref.1, bf16[512,512]{1,0:T(8,128)(2,1)} %vgr_ref.1, bf16[512,1024]{1,0:T(8,128)(2,1)} %res_ref.1, bf16[64,2048]{1,0:T(8,128)(2,1)} %wsh_ref.1, s32[1,512]{1,0:T(1,128)} %bitcast.2, s32[1,512]{1,0:T(1,128)} %bitcast.3), custom_call_target="tpu_custom_call" | custom-call | tf_op jit(solution)/shard_map/pallas_call | solution.py:473
  98.1 0.8 copy.9
  98.9 1.1 %convert_element_type.3 = f32[256,1024]{1,0:T(8,128)} convert(bf16[256,1024]{1,0:T(8,128)(2,1)S(1)} %get-tuple-element.5) | non-fusion elementwise | flops 262144 | bytes 1572864 | tf_op jit(solution)/shard_map/convert_element_type | solution.py:486

commit v6 on v5

--- a/solution.py
+++ b/solution.py
@@ -175,6 +175,11 @@
     def _():
         weights(4)
 
+    got(vg.at[1, :, cols(left)], v_r.at[1])
+    weight_tile(left)
+    got(vg.at[1, :, cols(right)], v_r.at[2])
+    weight_tile(right)
+
     across = (x + 2) % NX
     got(vg.at[0, top, cols(across)], x_r.at[4])
     send(vg.at[0, top, cols(across)], vg.at[1, top, cols(across)], v_s.at[0], v_r.at[3], partner)
@@ -199,9 +204,7 @@
             acc[b, :, start : start + size] += dot(vg[b, :, cols(q)], w[start : start + size, cols(q)], ((1,), (1,)))
 
     back_tile(x)
-    got(vg.at[1, :, cols(left)], v_r.at[1])
     back_tile(left)
-    got(vg.at[1, :, cols(right)], v_r.at[2])
     back_tile(right)
     got(vg.at[1, :, cols(across)], v_r.at[3])
 
@@ -278,14 +281,12 @@
             to = after if way == 0 else before
             send(gt[h].at[way], gr[h].at[way], n_s.at[h], n_r.at[2 * h + way], to)
 
-    pack(0)
-    weight_tile(left)
-    weight_tile(right)
     weight_tile(across)
     for way in range(2):
         start(way, 0, way)
     for way in range(2):
         start(way, 1, 1 - way)
+    pack(0)
     pack(1)
     for s in range(1, 4):
         if s == 2:

time: 101 us -> 102 us (level)
  Pallas kernels: 97.5 us -> 99.4 us
    pallas_call x1, Pallas kernels: 97.5 us -> 99.4 us  [body(): pl.pallas_call(kernel, out_shape=(pltpu.VMEM((ROWS, WIDTH), F32), pltpu.V...]
where the time goes in v6:
time: 102 us
  Pallas kernels  99.4 us (97%)
  other arithmetic  1.08 us (1%)
    pallas_call x1, Pallas kernels, body(): pl.pallas_call(kernel, out_shape=(pltpu.VMEM((ROWS, WIDTH), F32), pltpu.V...  99.4 us

profile of v6, /device:TPU:1, one launch (start us, length us, event | category | flops | bytes accessed | tf_op | source)
XLA Modules:
  0.0 101.9 jit_solution(13895430505055657228)
XLA Ops:
  0.6 99.4 %shard_map.77 = (f32[64,2048]{1,0:T(8,128)S(1)}, bf16[256,1024]{1,0:T(8,128)(2,1)S(1)}) custom-call(bf16[512,1024]{1,0:T(8,128)(2,1)} %li_ref.1, bf16[512,512]{1,0:T(8,128)(2,1)} %vgr_ref.1, bf16[512,1024]{1,0:T(8,128)(2,1)} %res_ref.1, bf16[64,2048]{1,0:T(8,128)(2,1)} %wsh_ref.1, s32[1,512]{1,0:T(1,128)} %bitcast.2, s32[1,512]{1,0:T(1,128)} %bitcast.3), custom_call_target="tpu_custom_call" | custom-call | tf_op jit(solution)/shard_map/pallas_call | solution.py:474
  100.0 0.8 copy.9
  100.8 1.1 %convert_element_type.3 = f32[256,1024]{1,0:T(8,128)} convert(bf16[256,1024]{1,0:T(8,128)(2,1)S(1)} %get-tuple-element.5) | non-fusion elementwise | flops 262144 | bytes 1572864 | tf_op jit(solution)/shard_map/convert_element_type | solution.py:487
